TPU v7x, 32 devices: a whole 2x2x4 slice. The times are simulated.
32 devices in a mesh: stream: 2 (over y), pages: 16 (over z, x, core).
Axes of the slice: x: 2, y: 2, z: 4, core: 2. Of those that a mesh axis runs over, the one named last changes fastest.
Arguments:
- features: bfloat16 [2, 16384, 768], P('stream', 'pages'), may hold values from -6 to 6
- box_bins: int32 [2, 3, 16384], P('stream', None, 'pages'), may hold values from 0 to 15
- text_mask: int32 [16384], P('pages'), may hold values from 0 to 1, as said below
- spatial_table: bfloat16 [256, 768], replicated, may hold values from -6 to 6
- joint_projection: bfloat16 [2, 768, 2304], P('stream', 'pages'), may hold values from -0.21875 to 0.21875
- spatial_projection: bfloat16 [2, 768, 1536], P('stream', 'pages'), may hold values from -0.21875 to 0.21875
- relative_table: float32 [2, 12, 93], P('stream'), may hold values from -3 to 3
- output_projection: bfloat16 [2, 768, 768], P('stream', 'pages'), may hold values from -1.75 to 1.75
- output_bias: float32 [2, 768], P('stream'), may hold values from -2 to 2
- norm_one_gain: float32 [2, 768], P('stream'), may hold values from 0.5 to 1.5
- norm_one_shift: float32 [2, 768], P('stream'), may hold values from -2 to 2
- up_weight: bfloat16 [2, 768, 3072], P('stream', 'pages'), may hold values from -0.21875 to 0.21875
- up_bias: float32 [2, 3072], P('stream'), may hold values from -3 to 3
- down_weight: bfloat16 [2, 3072, 768], P('stream', 'pages'), may hold values from -0.109375 to 0.109375
- down_bias: float32 [2, 768], P('stream'), may hold values from -2 to 2
- norm_two_gain: float32 [2, 768], P('stream'), may hold values from 0.5 to 1.5
- norm_two_shift: float32 [2, 768], P('stream'), may hold values from -2 to 2
- output_cotangent: bfloat16 [2, 16384, 768], P('stream', 'pages'), may hold values from -6 to 6
Outputs:
- layer_output: bfloat16 [2, 16384, 768], P('stream', 'pages')
- grad_features: float32 [2, 16384, 768], P('stream', 'pages')
- grad_joint: float32 [2, 768, 2304], P('stream', 'pages')
- grad_spatial: float32 [2, 768, 1536], P('stream', 'pages')
- grad_relative: float32 [2, 12, 93], P('stream')
- grad_output_projection: float32 [2, 768, 768], P('stream', 'pages')
- grad_output_bias: float32 [2, 768], P('stream')
- grad_norm_one_gain: float32 [2, 768], P('stream')
- grad_norm_one_shift: float32 [2, 768], P('stream')
- grad_up_weight: float32 [2, 768, 3072], P('stream', 'pages')
- grad_up_bias: float32 [2, 3072], P('stream')
- grad_down_weight: float32 [2, 3072, 768], P('stream', 'pages')
- grad_down_bias: float32 [2, 768], P('stream')
- grad_norm_two_gain: float32 [2, 768], P('stream')
- grad_norm_two_shift: float32 [2, 768], P('stream')
- grad_table: float32 [256, 768], replicated
Inputs may be any that keep to these rules, and one draw needn't show every extreme that they name: `text_mask`: each page of 512 consecutive slots is 1 on its first 20 to 512 slots and 0 after; in every draw one page is all ones and one has exactly 20 ones.
All inputs are finite; a program needn't handle non-finite values.
Results may differ from a plain program's by a relative error of at most 0.018.
Values may be sent and summed in bfloat16 or wider, within the bound.
No kernel may reach another device: no remote copies, remote signals or barrier semaphores. Data moves between devices by JAX's collectives and lax.ppermute only.
A program may use at most 256 MiB of HBM per device.

v0:
```python
import jax
import jax.numpy as jnp
from jax import lax
from jax.sharding import PartitionSpec as P

SLOTS = 512
BINS = 16
MICRO = 2


highest = lax.Precision.HIGHEST
epsilon = 1e-05
masked_score = -1000000000.0


def to_half(array):
    return array.astype(jnp.bfloat16)


def times(left_part, right_part):
    return jnp.dot(left_part, right_part, preferred_element_type=jnp.float32)


def times_over_rows(left_part, right_part):
    return lax.dot_general(
        left_part, right_part, (((0,), (0,)), ((), ())), preferred_element_type=jnp.float32
    )


def times_transposed(left_part, right_part):
    return lax.dot_general(
        left_part, right_part, (((1,), (1,)), ((), ())), preferred_element_type=jnp.float32
    )


def spatial_weight_grad(table_float, cell_grads):
    return lax.dot_general(table_float, cell_grads, (((0,), (0,)), ((), ())), precision=highest)


def layer_stats(values):
    centered = values - jnp.mean(values, -1, keepdims=True)
    inverse = lax.rsqrt(jnp.mean(centered * centered, -1, keepdims=True) + epsilon)
    return (centered * inverse, inverse)


def norm_back(grad_normed, normed, inverse):
    return inverse * (
        grad_normed
        - jnp.mean(grad_normed, -1, keepdims=True)
        - normed * jnp.mean(grad_normed * normed, -1, keepdims=True)
    )


def gelu_slope(values):
    cumulative = 0.5 * (1.0 + lax.erf(values * 0.7071067811865476))
    density = jnp.exp(-0.5 * values * values) * 0.3989422804014327
    return (values * cumulative, cumulative + values * density)


def offset_table():
    span_width = 2 * BINS - 1
    grid_shape = (BINS, BINS, span_width)
    row_bin = lax.broadcasted_iota(jnp.int32, grid_shape, 0)
    col_bin = lax.broadcasted_iota(jnp.int32, grid_shape, 1)
    offset = lax.broadcasted_iota(jnp.int32, grid_shape, 2)
    return (col_bin - row_bin + BINS - 1 == offset).astype(jnp.float32)


def pair_rows(relative, page_bins, offsets):
    span_width = 2 * BINS - 1
    slot_count = page_bins.shape[1]
    levels = lax.broadcasted_iota(jnp.int32, (3, BINS, slot_count), 1)
    onehot = (page_bins[:, None, :] == levels).astype(jnp.float32).reshape(3 * BINS, slot_count)
    left_parts = []
    for family in range(3):
        table_part = relative[:, family * span_width : (family + 1) * span_width]
        square = jnp.einsum("hr,acr->hac", table_part, offsets, precision=highest)
        left_parts.append(
            jnp.einsum(
                "ai,hac->ihc",
                onehot[family * BINS : (family + 1) * BINS],
                square,
                precision=highest,
            )
        )
    return (jnp.concatenate(left_parts, -1), onehot)


def page_scores(queries, key_rows, page_bins, key_valid, relative, offsets):
    score_scale = (queries.shape[-1] // 2) ** (-0.5)
    bias_rows, onehot = pair_rows(relative, page_bins, offsets)
    lifted_rows = bias_rows / score_scale
    top_part = to_half(lifted_rows)
    rest_part = lifted_rows - top_part.astype(jnp.float32)
    mid_part = to_half(rest_part)
    low_part = to_half(rest_part - mid_part.astype(jnp.float32))
    query_extra = jnp.concatenate([top_part, mid_part, low_part], -1)
    onehot_half = to_half(jnp.transpose(onehot))
    key_line = jnp.concatenate([onehot_half, onehot_half, onehot_half], -1)
    key_extra = jnp.broadcast_to(
        key_line[:, None, :], (key_line.shape[0], queries.shape[1], key_line.shape[1])
    )
    wide_queries = jnp.concatenate([queries, query_extra], -1)
    wide_keys = jnp.concatenate([key_rows, key_extra], -1)
    scores = (
        jnp.einsum("ihe,jhe->hij", wide_queries, wide_keys, preferred_element_type=jnp.float32)
        * score_scale
    )
    return (jnp.where(key_valid[None, None, :] > 0, scores, masked_score), onehot, score_scale)


def attend_page(page_items, relative, offsets):
    queries, key_rows, values, page_bins, key_valid = page_items
    scores, onehot, score_scale = page_scores(
        queries, key_rows, page_bins, key_valid, relative, offsets
    )
    largest = jnp.max(scores, -1, keepdims=True)
    lifted = jnp.exp(scores - largest)
    sum_total = jnp.sum(lifted, -1, keepdims=True)
    shares = to_half(lifted / sum_total)
    mixture = jnp.einsum("hij,jhe->ihe", shares, values, preferred_element_type=jnp.float32)
    return (to_half(mixture.reshape(mixture.shape[0], -1)), largest + jnp.log(sum_total))


def attend_back(page_items, relative, offsets):
    queries, key_rows, values, grad_mixture, log_total, page_bins, key_valid = page_items
    scores, onehot, score_scale = page_scores(
        queries, key_rows, page_bins, key_valid, relative, offsets
    )
    shares = jnp.exp(scores - log_total)
    grad_shares = jnp.einsum(
        "ihe,jhe->hij", grad_mixture, values, preferred_element_type=jnp.float32
    )
    grad_scores = to_half(shares * (grad_shares - jnp.sum(shares * grad_shares, -1, keepdims=True)))
    grad_queries = (
        jnp.einsum("hij,jhe->ihe", grad_scores, key_rows, preferred_element_type=jnp.float32)
        * score_scale
    )
    grad_keys = (
        jnp.einsum("hij,ihe->jhe", grad_scores, queries, preferred_element_type=jnp.float32)
        * score_scale
    )
    grad_values = jnp.einsum(
        "hij,ihe->jhe", to_half(shares), grad_mixture, preferred_element_type=jnp.float32
    )
    per_bin = jnp.einsum(
        "ci,hij->hcj", to_half(onehot), grad_scores, preferred_element_type=jnp.float32
    )
    pair_sums = jnp.einsum("hcj,dj->hcd", per_bin, onehot, precision=highest)
    pieces = []
    for family in range(3):
        block_sums = pair_sums[
            :, family * BINS : (family + 1) * BINS, family * BINS : (family + 1) * BINS
        ]
        pieces.append(jnp.einsum("hac,acr->hr", block_sums, offsets, precision=highest))
    return (grad_queries, grad_keys, grad_values, jnp.concatenate(pieces, -1))


def body(
    features,
    box_bins,
    text_mask,
    spatial_table,
    joint_projection,
    spatial_projection,
    relative_table,
    output_projection,
    output_bias,
    norm_one_gain,
    norm_one_shift,
    up_weight,
    up_bias,
    down_weight,
    down_bias,
    norm_two_gain,
    norm_two_shift,
    output_cotangent,
):
    float_type = jnp.float32
    width = features.shape[2]
    hidden_width = up_weight.shape[2]
    heads_count = relative_table.shape[1]
    head_size = width // heads_count
    block_rows = features.shape[1] // MICRO
    page_count = block_rows // SLOTS
    stream_side = lax.axis_index("stream")
    key_valid = jnp.where(stream_side == 0, text_mask, jnp.ones_like(text_mask))
    offsets = offset_table()
    relative = relative_table[0]
    gain_one = norm_one_gain[0]
    shift_one = norm_one_shift[0]
    gain_two = norm_two_gain[0]
    shift_two = norm_two_shift[0]
    bias_out = output_bias[0]
    bias_up = up_bias[0]
    bias_down = down_bias[0]
    table_float = spatial_table.astype(float_type)
    shards = (joint_projection, spatial_projection, output_projection, up_weight, down_weight)

    def split_heads(array):
        return array.reshape(array.shape[0], heads_count, -1)

    def by_page(array):
        return array.reshape((page_count, SLOTS) + array.shape[1:])

    def forward_page(page_items):
        return attend_page(page_items, relative, offsets)

    def backward_page(page_items):
        return attend_back(page_items, relative, offsets)

    zero_row = jnp.zeros((width,), float_type)
    grad_gain_one = zero_row
    grad_shift_one = zero_row
    grad_gain_two = zero_row
    grad_shift_two = zero_row
    grad_bias_out = zero_row
    grad_bias_down = zero_row
    grad_bias_up = jnp.zeros((hidden_width,), float_type)
    grad_relative = jnp.zeros_like(relative)
    spatial_total = jnp.zeros((spatial_table.shape[0], 2 * width), float_type)
    weight_grads = tuple((jnp.zeros(piece.shape, float_type) for piece in shards))
    layer_rows = []
    input_grads = []
    held = (
        lax.all_gather(joint_projection, "pages", axis=1, tiled=True),
        lax.all_gather(spatial_projection, "pages", axis=1, tiled=True),
        lax.all_gather(output_projection, "pages", axis=1, tiled=True),
        lax.all_gather(up_weight, "pages", axis=1, tiled=True),
        lax.all_gather(down_weight, "pages", axis=1, tiled=True),
    )
    for micro_index in range(MICRO):
        full_joint, full_spatial, full_output, full_up, full_down = [piece[0] for piece in held]
        if micro_index == 0:
            spatial_rows = to_half(times(spatial_table, full_spatial))
        first_row = micro_index * block_rows
        last_row = first_row + block_rows
        inputs = features[0, first_row:last_row]
        block_bins = box_bins[0, :, first_row:last_row]
        block_valid = key_valid[first_row:last_row]
        cell_ids = block_bins[2] * BINS + block_bins[1]
        spatial_tokens = jnp.take(spatial_rows, cell_ids, axis=0)
        joint_half = to_half(times(inputs, full_joint))
        queries = jnp.concatenate(
            [split_heads(joint_half[:, :width]), split_heads(spatial_tokens[:, :width])], -1
        )
        key_rows = jnp.concatenate(
            [split_heads(joint_half[:, width : 2 * width]), split_heads(spatial_tokens[:, width:])],
            -1,
        )
        values = split_heads(joint_half[:, 2 * width :])
        page_bins = jnp.transpose(block_bins.reshape(3, page_count, SLOTS), (1, 0, 2))
        mixture, log_total = lax.map(
            forward_page,
            (by_page(queries), by_page(key_rows), by_page(values), page_bins, by_page(block_valid)),
        )
        mixture = mixture.reshape(block_rows, width)
        attention_out = times(mixture, full_output) + bias_out
        joined = lax.psum(attention_out, "stream")
        normed_one, inverse_one = layer_stats(inputs.astype(float_type) + joined)
        hidden = normed_one * gain_one + shift_one
        hidden_half = to_half(hidden)
        activated, slope = gelu_slope(times(hidden_half, full_up) + bias_up)
        active_half = to_half(activated)
        normed_two, inverse_two = layer_stats(hidden + (times(active_half, full_down) + bias_down))
        layer_rows.append(to_half(normed_two * gain_two + shift_two))
        upstream = output_cotangent[0, first_row:last_row].astype(float_type)
        grad_gain_two = grad_gain_two + jnp.sum(upstream * normed_two, 0)
        grad_shift_two = grad_shift_two + jnp.sum(upstream, 0)
        grad_resid_two = norm_back(upstream * gain_two, normed_two, inverse_two)
        grad_branch = to_half(grad_resid_two)
        grad_bias_down = grad_bias_down + jnp.sum(grad_branch.astype(float_type), 0)
        grad_pre = to_half(times_transposed(grad_branch, full_down) * slope)
        grad_bias_up = grad_bias_up + jnp.sum(grad_pre.astype(float_type), 0)
        grad_hidden = grad_resid_two + times_transposed(grad_pre, full_up)
        grad_gain_one = grad_gain_one + jnp.sum(grad_hidden * normed_one, 0)
        grad_shift_one = grad_shift_one + jnp.sum(grad_hidden, 0)
        grad_resid_one = norm_back(grad_hidden * gain_one, normed_one, inverse_one)
        grad_joined = lax.psum(grad_resid_one, "stream")
        grad_attention = to_half(grad_joined)
        grad_bias_out = grad_bias_out + jnp.sum(grad_attention.astype(float_type), 0)
        grad_mixture = to_half(times_transposed(grad_attention, full_output))
        grad_queries, grad_keys, grad_values, relative_part = lax.map(
            backward_page,
            (
                by_page(queries),
                by_page(key_rows),
                by_page(values),
                by_page(split_heads(grad_mixture)),
                log_total,
                page_bins,
                by_page(block_valid),
            ),
        )
        grad_relative = grad_relative + jnp.sum(relative_part, 0)
        grad_queries = grad_queries.reshape(block_rows, heads_count, 2 * head_size)
        grad_keys = grad_keys.reshape(block_rows, heads_count, 2 * head_size)
        grad_joint_half = to_half(
            jnp.concatenate(
                [
                    grad_queries[..., :head_size].reshape(block_rows, width),
                    grad_keys[..., :head_size].reshape(block_rows, width),
                    grad_values.reshape(block_rows, width),
                ],
                1,
            )
        )
        grad_spatial_half = to_half(
            jnp.concatenate(
                [
                    grad_queries[..., head_size:].reshape(block_rows, width),
                    grad_keys[..., head_size:].reshape(block_rows, width),
                ],
                1,
            )
        )
        input_grads.append(grad_resid_one + times_transposed(grad_joint_half, full_joint))
        spatial_block = jax.ops.segment_sum(
            grad_spatial_half.astype(float_type), cell_ids, num_segments=spatial_table.shape[0]
        )
        spatial_total = spatial_total + spatial_block
        local_grads = (
            times_over_rows(inputs, grad_joint_half),
            times_over_rows(mixture, grad_attention),
            times_over_rows(hidden_half, grad_pre),
            times_over_rows(active_half, grad_branch),
        )
        spatial_grad = spatial_weight_grad(table_float, spatial_block)
        received = (
            lax.psum_scatter(local_grads[0][None], "pages", scatter_dimension=1, tiled=True),
            lax.psum_scatter(spatial_grad[None], "pages", scatter_dimension=1, tiled=True),
            lax.psum_scatter(local_grads[1][None], "pages", scatter_dimension=1, tiled=True),
            lax.psum_scatter(local_grads[2][None], "pages", scatter_dimension=1, tiled=True),
            lax.psum_scatter(local_grads[3][None], "pages", scatter_dimension=1, tiled=True),
        )
        weight_grads = tuple((earlier + latest for earlier, latest in zip(weight_grads, received)))
    table_part = lax.dot_general(
        spatial_total, full_spatial.astype(float_type), (((1,), (1,)), ((), ())), precision=highest
    )
    summed = lax.psum(
        (
            grad_gain_one,
            grad_shift_one,
            grad_bias_out,
            grad_bias_up,
            grad_bias_down,
            grad_gain_two,
            grad_shift_two,
            grad_relative,
            table_part,
        ),
        "pages",
    )
    grad_table = lax.psum(summed[8].astype(jnp.bfloat16), "stream").astype(jnp.float32)
    return (
        jnp.concatenate(layer_rows, 0)[None],
        jnp.concatenate(input_grads, 0)[None],
        weight_grads[0],
        weight_grads[1],
        summed[7][None],
        weight_grads[2],
        summed[2][None],
        summed[0][None],
        summed[1][None],
        weight_grads[3],
        summed[3][None],
        weight_grads[4],
        summed[4][None],
        summed[5][None],
        summed[6][None],
        grad_table,
    )


def solution(mesh):
    placed = (
        P("stream", "pages", None),
        P("stream", None, "pages"),
        P("pages"),
        P(),
        P("stream", "pages", None),
        P("stream", "pages", None),
        P("stream", None, None),
        P("stream", "pages", None),
        P("stream", None),
        P("stream", None),
        P("stream", None),
        P("stream", "pages", None),
        P("stream", None),
        P("stream", "pages", None),
        P("stream", None),
        P("stream", None),
        P("stream", None),
        P("stream", "pages", None),
    )
    return jax.shard_map(
        body,
        mesh=mesh,
        in_specs=placed,
        out_specs=(
            P("stream", "pages", None),
            P("stream", "pages", None),
            P("stream", "pages", None),
            P("stream", "pages", None),
            P("stream", None, None),
            P("stream", "pages", None),
            P("stream", None),
            P("stream", None),
            P("stream", None),
            P("stream", "pages", None),
            P("stream", None),
            P("stream", "pages", None),
            P("stream", None),
            P("stream", None),
            P("stream", None),
            P(),
        ),
        check_vma=False,
    )
```

profile of v0, /device:TPU:8, one launch (start us, length us, event | category | flops | bytes accessed | tf_op | source)
XLA Modules:
  0.0 1247.0 jit_solution(12594459284380180430)
XLA Ops:
  18.2 34.9 %all-gather.8.cloned.1.call-done = bf16[1,768,1536]{2,1,0:T(8,128)(2,1)} async-done(((bf16[1,48,1536]{2,1,0:T(8,128)(2,1)}), bf16[1,768,1536]{2,1,0:T(8,128)(2,1)}) %all-gather.8.cloned.1.call-update) | async-done | bytes 2359312 | tf_op jit(solution)/shard_map/all_gather | solution.py:227
  53.1 2.4 convolution_convert_fusion.2
  55.5 2.9 gather_fusion.1
  61.3 2.3 copy.132
  63.7 3.1 gather_fusion
  69.6 2.4 copy.123
  75.5 26.6 %all-gather.6.cloned.1.call-done = bf16[1,768,2304]{2,1,0:T(8,128)(2,1)} async-done(((bf16[1,48,2304]{2,1,0:T(8,128)(2,1)}), bf16[1,768,2304]{2,1,0:T(8,128)(2,1)}) %all-gather.6.cloned.1.call-update) | async-done | bytes 3538960 | tf_op jit(solution)/shard_map/all_gather | solution.py:226
  102.1 4.2 convolution_convert_fusion
  112.6 4.5 convolution_convert_fusion.1
  123.2 2.3 copy.116
  132.3 6.2 fusion.227
  140.6 2.5 copy-done.1
  143.2 2.5 fusion.132
  145.9 6.3 fusion.228
  154.1 2.7 copy-done.2
  157.0 2.4 fusion.133
  159.4 3.5 convolution_add_fusion
  170.0 79.4 %all-reduce.16.cloned.1.call-done = (f32[512,768]{1,0:T(8,128)}, f32[512,768]{1,0:T(8,128)}) async-done(((f32[512,768]{1,0:T(8,128)}, f32[512,768]{1,0:T(8,128)}), (f32[512,768]{1,0:T(8,128)}, f32[512,768]{1,0:T(8,128)})) %all-reduce.16.cloned.1.call-update) | async-done | bytes 3145744 | tf_op jit(solution)/shard_map/psum | solution.py:259
  249.4 2.7 fusion.214
  254.8 49.9 %all-gather.12.cloned.1.call-done = bf16[1,768,3072]{2,1,0:T(8,128)(2,1)} async-done(((bf16[1,48,3072]{2,1,0:T(8,128)(2,1)}), bf16[1,768,3072]{2,1,0:T(8,128)(2,1)}) %all-gather.12.cloned.1.call-update) | async-done | bytes 4718608 | tf_op jit(solution)/shard_map/all_gather | solution.py:229
  304.7 4.8 fusion.34
  309.6 2.7 copy-done.127
  312.3 7.5 multiply_convert_fusion.3
  319.8 38.8 %all-gather.14.cloned.1.call-done = bf16[1,3072,768]{2,1,0:T(8,128)(2,1)} async-done(((bf16[1,192,768]{2,1,0:T(8,128)(2,1)}), bf16[1,3072,768]{2,1,0:T(8,128)(2,1)}) %all-gather.14.cloned.1.call-update) | async-done | bytes 4718608 | tf_op jit(solution)/shard_map/all_gather | solution.py:230
  358.6 6.6 fusion.229
  365.6 2.8 fusion.230
  370.9 3.0 convert_reduce_fusion.4
  374.0 8.3 convert_reduce_fusion.1
  382.3 4.8 multiply_reduce_fusion.3
  387.1 5.3 convert_reduce_fusion
  392.5 7.0 multiply_reduce_fusion.2
  399.9 78.0 %all-reduce.17 = (bf16[512,768]{1,0:T(8,128)(2,1)}, bf16[512,768]{1,0:T(8,128)(2,1)}) all-reduce(f32[512,768]{1,0:T(8,128)S(1)} %subtract_multiply_fusion, f32[512,768]{1,0:T(8,128)} %get-tuple-element.293), channel_id=1, replica_groups=mesh['stream'=2,'pages'=16] {'stream'}, use_global_device_ids=true, to_apply=%region_24.26 | all-reduce | flops 786432 | bytes 4718592 | tf_op jit(solution)/shard_map/psum | solution.py:279
  479.2 3.2 convolution_convert_fusion.4
  483.9 7.6 fusion.126
  491.5 9.2 multiply_reduce_fusion.1
  500.7 7.0 multiply_convert_fusion.1
  507.7 3.3 fusion.101
  515.1 7.7 fusion.129
  522.8 9.0 multiply_reduce_fusion
  531.8 7.4 multiply_convert_fusion
  539.2 3.3 fusion.107
  554.2 2.4 fusion.221
  559.5 7.0 scatter_custom_fusion
  566.6 4.6 fusion.231
  571.2 4.7 convolution_bitcast_fusion
  579.5 2.3 copy.145
  581.9 2.6 fusion.219
  584.5 3.5 fusion.140
  588.0 5.0 add_bitcast_fusion.2
  592.9 16.9 %copy.142 = f32[1,768,2304]{2,0,1:T(1,128)} copy(f32[1,768,2304]{1,2,0:T(8,128)} %add_bitcast_fusion.2) | data formatting | bytes 14155776 | tf_op jit(solution)/shard_map/add | solution.py:336
  612.1 7.7 scatter_custom_fusion.1
  619.9 5.3 fusion.58
  627.1 59.6 %all-reduce.18 = (f32[1,12,93]{2,1,0:T(8,128)}, f32[1,768]{1,0:T(1,128)}, f32[1,768]{1,0:T(1,128)}, f32[1,768]{1,0:T(1,128)}, f32[1,3072]{1,0:T(1,128)}, /*index...) all-reduce(f32[1,12,93]{2,1,0:T(8,128)} %fusion.177, ...), channel_id=1, replica_groups=mesh['stream'=2,'pages'=16] {'pages'}, use_global_device_ids=true, to_apply=%region_32.34 | all-reduce | flops 205404 | bytes 1250016 | tf_op jit(solution)/shard_map/psum | solution.py:340
  686.8 6.9 add_bitcast_fusion.3
  693.7 12.2 copy.147
  712.8 5.0 fusion.209
  717.8 5.7 add_bitcast_fusion.1
  725.0 4.8 fusion.195
  729.8 5.3 add_bitcast_fusion
  738.9 4.5 fusion.110
  749.3 192.7 %all-reduce.14.cloned.1.call-done = (f32[1,768,2304]{2,0,1:T(1,128)}, f32[1,768,1536]{2,0,1:T(1,128)}) async-done(((f32[1,768,2304]{2,0,1:T(1,128)}, f32[1,768,1536]{2,0,1:T(1,128)}), (f32[1,768,2304]{2,0,1:T(1,128)}, f32[1,768,1536]{2,0,1:T(1,128)})) %all-reduce.14.cloned.1.call-update) | async-done | bytes 11796496
  945.5 63.8 %reduce-scatter.4.cloned.1.call-done = f32[1,48,768]{2,1,0:T(8,128)} async-done(((f32[1,768,768]{2,1,0:T(8,128)}), f32[1,48,768]{2,1,0:T(8,128)}) %reduce-scatter.4.cloned.1.call-update) | async-done | bytes 147472 | tf_op jit(solution)/shard_map/reduce_scatter | solution.py:332
  1009.4 115.1 %reduce-scatter.6.cloned.1.call-done = f32[1,48,3072]{2,1,0:T(8,128)} async-done(((f32[1,768,3072]{2,1,0:T(8,128)}), f32[1,48,3072]{2,1,0:T(8,128)}) %reduce-scatter.6.cloned.1.call-update) | async-done | bytes 589840 | tf_op jit(solution)/shard_map/reduce_scatter | solution.py:333
  1124.5 115.5 %reduce-scatter.8.cloned.1.call-done = f32[1,192,768]{2,1,0:T(8,128)} async-done(((f32[1,3072,768]{2,1,0:T(8,128)}), f32[1,192,768]{2,1,0:T(8,128)}) %reduce-scatter.8.cloned.1.call-update) | async-done | bytes 589840 | tf_op jit(solution)/shard_map/reduce_scatter | solution.py:334
  (446 shorter events, 106.1 us)
Async XLA Ops:
  7.2 45.9 %copy-start = (bf16[256,768]{1,0:T(8,128)(2,1)S(1)}, bf16[256,768]{1,0:T(8,128)(2,1)}, u32[]{:S(2)}) copy-start(bf16[256,768]{1,0:T(8,128)(2,1)} %param.23) | copy-start | bytes 1179652
  7.2 8.3 copy-start.107
  7.2 45.9 %all-gather.8.cloned.1.call-start = ((), (), s32[]{:S(2)}) async-start(), calls=%async_computation.4 | async-start | bytes 2506752 | tf_op jit(solution)/shard_map/all_gather | solution.py:227
  7.9 94.2 %all-gather.6.cloned.1.call-start = ((), (), s32[]{:S(2)}) async-start(), calls=%async_computation.3 | async-start | bytes 3760128 | tf_op jit(solution)/shard_map/all_gather | solution.py:226
  8.7 150.7 %all-gather.10.cloned.1.call-start = ((), (), s32[]{:S(2)}) async-start(), calls=%async_computation.5 | async-start | bytes 1253376 | tf_op jit(solution)/shard_map/all_gather | solution.py:228
  9.4 240.0 %all-reduce.16.cloned.1.call-start = ((), (), s32[]{:S(2)}) async-start(), calls=%async_computation.13 | async-start | bytes 6291456 | tf_op jit(solution)/shard_map/psum | solution.py:259
  12.4 5.7 copy-start.109
  112.6 28.0 %copy-start.19 = (bf16[512,768]{0,1:T(8,128)(2,1)}, bf16[512,768]{0,1:T(8,128)(2,1)S(1)}, u32[]{:S(2)}) copy-start(bf16[512,768]{0,1:T(8,128)(2,1)S(1)} %copy.125) | copy-start | bytes 2359300
  145.7 13.7 %copy-start.41 = (bf16[12,64,512]{2,1,0:T(8,128)(2,1)}, bf16[12,64,512]{2,1,0:T(8,128)(2,1)S(1)}, u32[]{:S(2)}) copy-start(bf16[12,64,512]{2,1,0:T(8,128)(2,1)S(1)} %fusion.132) | copy-start | bytes 2359300
  165.0 139.7 %all-gather.12.cloned.1.call-start = ((), (), s32[]{:S(2)}) async-start(), calls=%async_computation.6 | async-start | bytes 5013504 | tf_op jit(solution)/shard_map/all_gather | solution.py:229
  165.6 193.0 %all-gather.14.cloned.1.call-start = ((), (), s32[]{:S(2)}) async-start(), calls=%async_computation.7 | async-start | bytes 5013504 | tf_op jit(solution)/shard_map/all_gather | solution.py:230
  166.2 581.2 %all-reduce.12.cloned.1.call-start = ((), (), s32[]{:S(2)}) async-start(), calls=%async_computation.8 | async-start | bytes 786432 | tf_op jit(solution)/shard_map/psum | solution.py:354
  304.7 7.5 copy-start.14
  304.7 7.5 copy-start.96
  304.7 7.5 copy-start.115
  304.7 7.5 copy-start.119
  304.7 7.5 copy-start.124
  358.6 7.0 copy-start.7
  358.6 7.0 copy-start.82
  358.6 7.0 copy-start.108
  358.6 7.0 copy-start.120
  370.9 11.4 slice-start.8
  370.9 16.2 %slice-start.10 = ((s8[6291456]{0:T(1024)(128)(4,1)}), s8[4194304]{0:T(1024)(128)(4,1)S(1)}, s32[]{:S(2)}) async-start(s8[6291456]{0:T(1024)(128)(4,1)} %bitcast.427), calls=%async_computation.24 | async-start | bytes 8388608
  373.9 8.4 copy-start.11
  373.9 18.6 %copy-start.9 = (f32[512,768]{1,0:T(8,128)}, f32[512,768]{1,0:T(8,128)S(1)}, u32[]{:S(2)}) copy-start(f32[512,768]{1,0:T(8,128)S(1)} %get-tuple-element.243) | copy-start | bytes 4718596
  373.9 8.4 copy-start.15
  373.9 8.4 copy-start.97
  373.9 8.4 copy-start.116
  373.9 8.4 slice-start.9
  373.9 13.2 %slice-start.11 = ((s8[6291456]{0:T(1024)(128)(4,1)}), s8[2097152]{0:T(1024)(128)(4,1)S(1)}, s32[]{:S(2)}) async-start(s8[6291456]{0:T(1024)(128)(4,1)} %bitcast.427), calls=%async_computation.25 | async-start | bytes 4194304
  392.5 7.0 copy-start.23
  399.9 79.3 %copy-start.17 = (f32[512,768]{1,0:T(8,128)}, f32[512,768]{1,0:T(8,128)S(1)}, u32[]{:S(2)}) copy-start(f32[512,768]{1,0:T(8,128)S(1)} %subtract_multiply_fusion) | copy-start | bytes 4718596
  483.8 7.7 copy-start.22
  483.8 7.7 copy-start.65
  483.8 16.9 %slice-start.3 = ((s8[12582912]{0:T(1024)(128)(4,1)}), s8[4194304]{0:T(1024)(128)(4,1)S(1)}, s32[]{:S(2)}) async-start(s8[12582912]{0:T(1024)(128)(4,1)} %bitcast.340), calls=%async_computation.17 | async-start | bytes 8388608
  483.9 16.8 %slice-start.4 = ((s8[12582912]{0:T(1024)(128)(4,1)}), s8[4194304]{0:T(1024)(128)(4,1)S(1)}, s32[]{:S(2)}) async-start(s8[12582912]{0:T(1024)(128)(4,1)} %bitcast.340), calls=%async_computation.18 | async-start | bytes 8388608
  491.5 9.2 slice-start.5
  500.7 7.0 copy-start.33
  500.7 7.0 copy-start.34
  515.1 7.7 copy-start.20
  515.1 7.7 copy-start.64
  515.1 16.7 %slice-start = ((s8[12582912]{0:T(1024)(128)(4,1)}), s8[4194304]{0:T(1024)(128)(4,1)S(1)}, s32[]{:S(2)}) async-start(s8[12582912]{0:T(1024)(128)(4,1)} %bitcast.338), calls=%async_computation.14 | async-start | bytes 8388608
  515.1 16.6 %slice-start.1 = ((s8[12582912]{0:T(1024)(128)(4,1)}), s8[4194304]{0:T(1024)(128)(4,1)S(1)}, s32[]{:S(2)}) async-start(s8[12582912]{0:T(1024)(128)(4,1)} %bitcast.338), calls=%async_computation.15 | async-start | bytes 8388608
  522.8 9.0 slice-start.2
  531.8 7.4 copy-start.30
  531.8 7.4 copy-start.32
  539.2 9.1 slice-start.6
  543.1 5.2 slice-start.7
  619.9 5.3 copy-start.79
  619.9 5.6 copy-start.78
  619.9 5.9 copy-start.93
  619.9 5.9 copy-start.94
  619.9 6.6 copy-start.98
  619.9 6.5 copy-start.99
  619.9 6.5 copy-start.100
  619.9 6.5 copy-start.101
  619.9 7.2 copy-start.92
  625.2 61.6 %copy-start.6 = (f32[256,1536]{1,0:T(8,128)S(1)}, f32[256,1536]{1,0:T(8,128)}, u32[]{:S(2)}) copy-start(f32[256,1536]{1,0:T(8,128)} %scatter_custom_fusion.1) | copy-start | bytes 4718596
  686.7 255.2 %all-reduce.14.cloned.1.call-start = ((), (), s32[]{:S(2)}) async-start(), calls=%async_computation.12 | async-start | bytes 23592960
  706.0 303.4 %reduce-scatter.4.cloned.1.call-start = ((), (), s32[]{:S(2)}) async-start(), calls=%async_computation.9 | async-start | bytes 2506752 | tf_op jit(solution)/shard_map/reduce_scatter | solution.py:332
  711.4 6.4 copy-start.83
  711.4 413.1 %reduce-scatter.6.cloned.1.call-start = ((), (), s32[]{:S(2)}) async-start(), calls=%async_computation.10 | async-start | bytes 10027008 | tf_op jit(solution)/shard_map/reduce_scatter | solution.py:333
  723.6 6.2 copy-start.10
  723.6 516.4 %reduce-scatter.8.cloned.1.call-start = ((), (), s32[]{:S(2)}) async-start(), calls=%async_computation.11 | async-start | bytes 10027008 | tf_op jit(solution)/shard_map/reduce_scatter | solution.py:334
  (88 other events, 269.5 us)
Sparse Core Ops, SparseCore 0:
  10.3 42.7 all-gather.7
  55.4 46.7 all-gather.5
  104.4 35.5 all-gather.9
  165.1 84.2 all-reduce.15
  251.6 53.1 all-gather.11
  306.9 51.6 all-gather.13
  686.9 30.6 all-reduce.11
  721.3 220.6 all-reduce.13
  946.3 63.0 reduce-scatter.3
  1013.9 110.5 reduce-scatter.5
  1129.2 110.8 reduce-scatter.7
where the time goes:
time: 1250 us
  waiting for transfers between devices  720 us (58%)
  matrix products  201 us (16%)
  blocking collectives  138 us (11%)
  local copies, waits for them, and re-layouts  107 us (9%)
  other arithmetic  63 us (5%)
  between operations  16.8 us (1%)
    unnamed x12, waiting for transfers between devices  196 us
    reduce_scatter x1, waiting for transfers between devices, body(): lax.psum_scatter(local_grads[3][None], 'pages', scatter_dimension=1, tile...  116 us
    reduce_scatter x1, waiting for transfers between devices, body(): lax.psum_scatter(local_grads[2][None], 'pages', scatter_dimension=1, tile...  115 us
    psum x1, waiting for transfers between devices, body(): joined = lax.psum(attention_out, 'stream')  79.4 us
    psum x1, blocking collectives, body(): grad_joined = lax.psum(grad_resid_one, 'stream')  78 us
    reduce_scatter x1, waiting for transfers between devices, body(): lax.psum_scatter(local_grads[1][None], 'pages', scatter_dimension=1, tile...  63.8 us
    psum x1, blocking collectives, body(): lax.psum((grad_gain_one, grad_shift_one, grad_bias_out, grad_bias_up, gra...  59.6 us
    all_gather x1, waiting for transfers between devices, body(): lax.all_gather(up_weight, 'pages', axis=1, tiled=True)  49.9 us
  transfers between devices with their start and end apart: 11, of which 9 were waited for; matrix products, arithmetic and copies ran while one was open for 13% of the time, Pallas kernels for 0%

commit v1 on v0

v1 whole, which is shorter than its diff:
```python
import functools

import jax
import jax.numpy as jnp
from jax import lax
from jax.experimental import pallas as pl
from jax.experimental.pallas import tpu as pltpu
from jax.sharding import PartitionSpec as P

SLOTS = 512
BINS = 16
SPAN = 2 * BINS - 1
LEVELS = 3 * BINS
PAIR = 2
LANES = 128

highest = lax.Precision.HIGHEST
epsilon = 1e-05
masked_score = -1000000000.0
half = jnp.bfloat16
single = jnp.float32


def times(left, right):
    return jnp.dot(left, right, preferred_element_type=single)


def times_over_rows(left, right):
    return lax.dot_general(left, right, (((0,), (0,)), ((), ())), preferred_element_type=single)


def times_transposed(left, right):
    return lax.dot_general(left, right, (((1,), (1,)), ((), ())), preferred_element_type=single)


def layer_stats(values):
    centered = values - jnp.mean(values, -1, keepdims=True)
    inverse = lax.rsqrt(jnp.mean(centered * centered, -1, keepdims=True) + epsilon)
    return (centered * inverse, inverse)


def norm_back(grad_normed, normed, inverse):
    return inverse * (
        grad_normed
        - jnp.mean(grad_normed, -1, keepdims=True)
        - normed * jnp.mean(grad_normed * normed, -1, keepdims=True)
    )


def gelu_slope(values):
    cumulative = 0.5 * (1.0 + lax.erf(values * 0.7071067811865476))
    density = jnp.exp(-0.5 * values * values) * 0.3989422804014327
    return (values * cumulative, cumulative + values * density)


def flip(count, bit):
    return [(place, place ^ bit) for place in range(count)]


def swap_streams(array):
    return lax.ppermute(array, "stream", [(0, 1), (1, 0)])


def rounded(array, kept):
    return lax.reduce_precision(array, 8, 7) if kept == half else array


def bits_of(count):
    return [1 << step for step in range(count.bit_length() - 1)]


def sum_pages(array, count, kept):
    for bit in bits_of(count):
        array = rounded(array, kept)
        received = lax.ppermute(array.astype(kept), "pages", flip(count, bit))
        array = array + received.astype(array.dtype)
    return array


def grads_kernel(lhs_ref, rhs_ref, keep_ref, send_ref, tile_ref, sem, *, blocks, by_rows):
    place = lax.axis_index("pages")
    step = pl.program_id(0)
    rows, columns = tile_ref.shape[1] // blocks, tile_ref.shape[2]
    buffer = lax.rem(step, 2)
    lhs = lhs_ref[...]
    rhs = rhs_ref[...].reshape(rhs_ref.shape[-2:])

    def copies(at, action):
        for block in range(blocks):
            owner = at * blocks + block if by_rows else block
            column = 0 if by_rows else at * columns
            slot = place ^ owner
            index = ((slot >> 1) & 1) * 4 + (slot >> 2)
            source = tile_ref.at[lax.rem(at, 2), pl.ds(block * rows, rows)]

            def into(target):
                where = pl.ds(pl.multiple_of(column, LANES), columns)
                return pltpu.make_async_copy(
                    source, target.at[index, :, where], sem.at[lax.rem(at, 2), block]
                )

            @pl.when((slot & 1) == 0)
            def _():
                action(into(keep_ref))

            @pl.when((slot & 1) == 1)
            def _():
                action(into(send_ref))

    @pl.when(step >= 2)
    def _():
        copies(step - 2, lambda copy: copy.wait())

    tile_ref[buffer] = times_over_rows(lhs, rhs).astype(half)
    copies(step, lambda copy: copy.start())

    @pl.when(step == pl.num_programs(0) - 1)
    def _():
        @pl.when(step >= 1)
        def _():
            copies(step - 1, lambda copy: copy.wait())

        copies(step, lambda copy: copy.wait())


def weight_grads(lhs, rhs, count, tile, by_rows):
    rows_all = lhs.shape[1]
    columns = rhs.shape[1] if rhs.ndim == 2 else rhs.shape[0] * rhs.shape[2]
    rows = rows_all // count
    tokens = lhs.shape[0]
    if by_rows:
        steps, blocks, tile_shape = rows_all // tile, tile // rows, (tile, columns)
        lhs_spec = pl.BlockSpec((tokens, tile), lambda i: (0, i))
        rhs_spec = pl.BlockSpec((tokens, columns), lambda i: (0, 0))
    else:
        steps, blocks, tile_shape = columns // tile, count, (rows_all, tile)
        lhs_spec = pl.BlockSpec((tokens, rows_all), lambda i: (0, 0))
        rhs_spec = pl.BlockSpec((tokens, tile), lambda i: (0, i))
        if rhs.ndim == 3:
            rhs_spec = pl.BlockSpec((1, tokens, tile), lambda i: (i, 0, 0))
    out = jax.ShapeDtypeStruct((count // 2, rows, columns), half)
    return pl.pallas_call(
        functools.partial(grads_kernel, blocks=blocks, by_rows=by_rows),
        grid=(steps,),
        in_specs=[lhs_spec, rhs_spec],
        out_specs=[pl.BlockSpec(memory_space=pltpu.HBM)] * 2,
        out_shape=[out, out],
        scratch_shapes=[
            pltpu.VMEM((2, *tile_shape), half),
            pltpu.SemaphoreType.DMA((2, blocks)),
        ],
        compiler_params=pltpu.CompilerParams(vmem_limit_bytes=40 << 20),
        cost_estimate=pl.CostEstimate(
            flops=2 * tokens * rows_all * columns,
            bytes_accessed=2 * (tokens * (rows_all + columns) + rows_all * columns),
            transcendentals=0,
        ),
        name="weight_grads",
    )(lhs, rhs)


def scatter_sum(keep, send, count):
    received = lax.ppermute(send, "pages", flip(count, 1))
    quarter = keep.shape[0] // 2

    def added(part):
        return (keep[part].astype(single) + received[part].astype(single)).astype(half)

    send = added(slice(quarter, None))
    received_x = lax.ppermute(send, "pages", flip(count, 2))
    keep = added(slice(0, quarter))
    total = keep[0].astype(single) + received_x[0].astype(single)
    for slot in range(1, quarter):
        part = (keep[slot].astype(single) + received_x[slot].astype(single)).astype(half)
        total = total + lax.ppermute(part, "pages", flip(count, 4 * slot)).astype(single)
    return total


def summed_rows(lhs, rhs, count, tile, by_rows=False):
    if count == 16:
        return scatter_sum(*weight_grads(lhs, rhs, count, tile, by_rows), count)[None]
    if rhs.ndim == 3:
        rhs = jnp.concatenate(list(rhs), -1)
    local = times_over_rows(lhs, rhs).astype(half)
    return lax.psum_scatter(local[None], "pages", scatter_dimension=1, tiled=True).astype(single)


def wide_rows(first, second, extra, which, size):
    lanes = slice(which * size, (which + 1) * size)
    return jnp.concatenate([first[:, lanes], second[:, lanes], extra], axis=1)


def forward_kernel(
    q_ref, k_ref, v_ref, sq_ref, sk_ref, cells_ref, keyx_ref, rel_ref, out_w_ref, bias_ref,
    mix_ref, att_ref, send_ref, log_ref, *, scale, size
):
    pair = pl.program_id(0)
    cells = cells_ref[...]
    keyx = keyx_ref[...]
    q = (q_ref[...].astype(single) * scale).astype(half)
    sq = (times(cells, sq_ref[...]) * scale).astype(half)
    sk = times(cells, sk_ref[...]).astype(half)
    k = k_ref[...]
    values_t = jnp.transpose(v_ref[...])
    rel = times(keyx, rel_ref[...]).astype(half)
    mixed = []
    for which in range(PAIR):
        wide_q = wide_rows(q, sq, rel[:, which * LANES : (which + 1) * LANES], which, size)
        wide_k = wide_rows(k, sk, keyx, which, size)
        scores = times_transposed(wide_k, wide_q)
        largest = jnp.max(scores, 0, keepdims=True)
        lifted = jnp.exp(scores - largest)
        total = jnp.sum(lifted, 0, keepdims=True)
        log_ref[pl.ds(pair * PAIR + which, 1), :] = largest + jnp.log(total)
        part = times(values_t[which * size : (which + 1) * size], lifted.astype(half))
        mixed.append(part / total)
    mixture = jnp.transpose(jnp.concatenate(mixed, axis=0)).astype(half)
    mix_ref[...] = mixture

    @pl.when(pair == 0)
    def _():
        att_ref[...] = jnp.broadcast_to(bias_ref[...], att_ref.shape)

    att_ref[...] += times(mixture, out_w_ref[...])

    @pl.when(pair == pl.num_programs(0) - 1)
    def _():
        send_ref[...] = att_ref[...].astype(half)


def attend_page(page, joint_half, spatial_rows, cells, keyx, rel, out_w, bias, heads):
    width = out_w.shape[0]
    size = width // heads
    pairs = heads // PAIR
    block = PAIR * size
    table_rows = spatial_rows.shape[0]
    return pl.pallas_call(
        functools.partial(forward_kernel, scale=size**-0.5, size=size),
        grid=(pairs,),
        in_specs=[
            pl.BlockSpec((SLOTS, block), lambda h: (page, h)),
            pl.BlockSpec((SLOTS, block), lambda h: (page, pairs + h)),
            pl.BlockSpec((SLOTS, block), lambda h: (page, 2 * pairs + h)),
            pl.BlockSpec((table_rows, block), lambda h: (0, h)),
            pl.BlockSpec((table_rows, block), lambda h: (0, pairs + h)),
            pl.BlockSpec((SLOTS, table_rows), lambda h: (page, 0)),
            pl.BlockSpec((SLOTS, LANES), lambda h: (page, 0)),
            pl.BlockSpec((LANES, PAIR * LANES), lambda h: (0, h)),
            pl.BlockSpec((block, width), lambda h: (h, 0)),
            pl.BlockSpec((1, width), lambda h: (0, 0)),
        ],
        out_specs=[
            pl.BlockSpec((SLOTS, block), lambda h: (0, h)),
            pl.BlockSpec((SLOTS, width), lambda h: (0, 0)),
            pl.BlockSpec((SLOTS, width), lambda h: (0, 0)),
            pl.BlockSpec((heads, SLOTS), lambda h: (0, 0)),
        ],
        out_shape=[
            jax.ShapeDtypeStruct((SLOTS, width), half),
            jax.ShapeDtypeStruct((SLOTS, width), single),
            jax.ShapeDtypeStruct((SLOTS, width), half),
            jax.ShapeDtypeStruct((heads, SLOTS), single),
        ],
        compiler_params=pltpu.CompilerParams(vmem_limit_bytes=32 << 20),
        cost_estimate=pl.CostEstimate(
            flops=2 * heads * SLOTS * SLOTS * 6 * size,
            bytes_accessed=12 * SLOTS * width,
            transcendentals=heads * SLOTS * SLOTS,
        ),
        name="attend_page",
    )(
        joint_half, joint_half, joint_half, spatial_rows, spatial_rows, cells, keyx, rel, out_w,
        bias,
    )


def backward_kernel(
    q_ref, k_ref, v_ref, sq_ref, sk_ref, cells_ref, cells_t_ref, keyx_ref, rel_ref, log_ref,
    grad_ref, out_w_ref, *refs, scale, size, first
):
    if first:
        rows_ref, cell_q_ref, cell_k_ref, sums_ref = refs
    else:
        _, old_q_ref, old_k_ref, old_sums_ref, rows_ref, cell_q_ref, cell_k_ref, sums_ref = refs
    pair = pl.program_id(0)
    cells = cells_ref[...]
    cells_t = cells_t_ref[...]
    keyx = keyx_ref[...]
    q = (q_ref[...].astype(single) * scale).astype(half)
    sq = (times(cells, sq_ref[...]) * scale).astype(half)
    sk = times(cells, sk_ref[...]).astype(half)
    k = k_ref[...]
    v = v_ref[...]
    grad = times_transposed(grad_ref[...], out_w_ref[...]).astype(half)
    rel = times(keyx, rel_ref[...]).astype(half)
    gq, gsq, gk, gsk, gv = [], [], [], [], []
    for which in range(PAIR):
        lanes = slice(which * size, (which + 1) * size)
        wide_q = wide_rows(q, sq, rel[:, which * LANES : (which + 1) * LANES], which, size)
        wide_k = wide_rows(k, sk, keyx, which, size)
        scores = times_transposed(wide_k, wide_q)
        shares = jnp.exp(scores - log_ref[pl.ds(pair * PAIR + which, 1), :])
        grad_shares = times_transposed(v[:, lanes], grad[:, lanes])
        row_sums = jnp.sum(shares * grad_shares, 0, keepdims=True)
        grad_scores = (shares * (grad_shares - row_sums)).astype(half)
        gv.append(times(shares.astype(half), grad[:, lanes]))
        both = times(grad_scores, wide_q[:, : 2 * size])
        gk.append(both[:, :size])
        gsk.append(both[:, size:])
        wide_grad = times(jnp.transpose(wide_k), grad_scores)
        gq.append(wide_grad[:size] * scale)
        gsq.append(wide_grad[size : 2 * size] * scale)
        bins = wide_grad[2 * size : 2 * size + LEVELS]
        top = bins.astype(half)
        rest = (bins - top.astype(single)).astype(half)
        sums = times(top, keyx) + times(rest, keyx)
        part = slice(which * LEVELS, (which + 1) * LEVELS)
        sums_ref[0, part, :] = sums if first else sums + old_sums_ref[0, part, :]
    rows_ref[0] = jnp.transpose(jnp.concatenate(gq, axis=0)).astype(half)
    rows_ref[1] = jnp.concatenate(gk, axis=1).astype(half)
    rows_ref[2] = jnp.concatenate(gv, axis=1).astype(half)
    cell_q = times(cells_t, jnp.transpose(jnp.concatenate(gsq, axis=0)).astype(half))
    cell_k = times(cells_t, jnp.concatenate(gsk, axis=1).astype(half))
    cell_q_ref[...] = cell_q if first else cell_q + old_q_ref[...]
    cell_k_ref[...] = cell_k if first else cell_k + old_k_ref[...]


def attend_page_back(
    page, joint_half, spatial_rows, cells, cells_t, keyx, rel, log_total, grad, out_w, heads, before
):
    tokens = joint_half.shape[0]
    width = out_w.shape[0]
    size = width // heads
    pairs = heads // PAIR
    block = PAIR * size
    table_rows = spatial_rows.shape[0]
    cells_out = pl.BlockSpec((table_rows, block), lambda h: (0, h))
    sums_out = pl.BlockSpec((1, PAIR * LEVELS, LANES), lambda h: (h, 0, 0))
    first = before is None
    more = [] if first else [pl.BlockSpec(memory_space=pltpu.HBM), cells_out, cells_out, sums_out]
    return pl.pallas_call(
        functools.partial(backward_kernel, scale=size**-0.5, size=size, first=first),
        grid=(pairs,),
        in_specs=[
            pl.BlockSpec((SLOTS, block), lambda h: (page, h)),
            pl.BlockSpec((SLOTS, block), lambda h: (page, pairs + h)),
            pl.BlockSpec((SLOTS, block), lambda h: (page, 2 * pairs + h)),
            pl.BlockSpec((table_rows, block), lambda h: (0, h)),
            pl.BlockSpec((table_rows, block), lambda h: (0, pairs + h)),
            pl.BlockSpec((SLOTS, table_rows), lambda h: (page, 0)),
            pl.BlockSpec((table_rows, SLOTS), lambda h: (0, page)),
            pl.BlockSpec((SLOTS, LANES), lambda h: (page, 0)),
            pl.BlockSpec((LANES, PAIR * LANES), lambda h: (0, h)),
            pl.BlockSpec((heads, SLOTS), lambda h: (0, 0)),
            pl.BlockSpec((SLOTS, width), lambda h: (0, 0)),
            pl.BlockSpec((block, width), lambda h: (h, 0)),
            *more,
        ],
        out_specs=[
            pl.BlockSpec((3, SLOTS, block), lambda h: (0, page, h)), cells_out, cells_out, sums_out
        ],
        out_shape=[
            jax.ShapeDtypeStruct((3, tokens, width), half),
            jax.ShapeDtypeStruct((table_rows, width), single),
            jax.ShapeDtypeStruct((table_rows, width), single),
            jax.ShapeDtypeStruct((pairs, PAIR * LEVELS, LANES), single),
        ],
        input_output_aliases={} if first else {12: 0, 13: 1, 14: 2, 15: 3},
        compiler_params=pltpu.CompilerParams(vmem_limit_bytes=32 << 20),
        cost_estimate=pl.CostEstimate(
            flops=2 * heads * SLOTS * SLOTS * 16 * size,
            bytes_accessed=20 * SLOTS * width,
            transcendentals=heads * SLOTS * SLOTS,
        ),
        name="attend_page_back",
    )(
        joint_half, joint_half, joint_half, spatial_rows, spatial_rows, cells, cells_t, keyx, rel,
        log_total, grad, out_w, *(before or ()),
    )


def input_grad_kernel(rows_ref, weight_ref, resid_ref, out_ref):
    part = times_transposed(rows_ref[0], weight_ref[...])

    @pl.when(pl.program_id(0) == 0)
    def _():
        out_ref[...] = resid_ref[...] + part

    @pl.when(pl.program_id(0) > 0)
    def _():
        out_ref[...] += part


def input_grad(rows, weight, resid):
    parts, tokens, width = rows.shape
    return pl.pallas_call(
        input_grad_kernel,
        grid=(parts,),
        in_specs=[
            pl.BlockSpec((1, tokens, width), lambda n: (n, 0, 0)),
            pl.BlockSpec((width, width), lambda n: (0, n)),
            pl.BlockSpec((tokens, width), lambda n: (0, 0)),
        ],
        out_specs=pl.BlockSpec((tokens, width), lambda n: (0, 0)),
        out_shape=jax.ShapeDtypeStruct((tokens, width), single),
        compiler_params=pltpu.CompilerParams(vmem_limit_bytes=32 << 20),
        cost_estimate=pl.CostEstimate(
            flops=2 * parts * tokens * width * width,
            bytes_accessed=14 * tokens * width,
            transcendentals=0,
        ),
        name="input_grad",
    )(rows, weight, resid)


def level_offsets():
    row_bin = lax.broadcasted_iota(jnp.int32, (BINS, BINS, SPAN), 0)
    col_bin = lax.broadcasted_iota(jnp.int32, (BINS, BINS, SPAN), 1)
    offset = lax.broadcasted_iota(jnp.int32, (BINS, BINS, SPAN), 2)
    return (col_bin - row_bin + BINS - 1 == offset).astype(single)


def relative_columns(relative, offsets):
    heads = relative.shape[0]
    tables = relative.reshape(heads, 3, SPAN)
    squares = jnp.einsum("hfr,acr->fahc", tables, offsets, precision=highest)
    blocks = jnp.zeros((3, BINS, heads, 3, BINS), single)
    for family in range(3):
        blocks = blocks.at[family, :, :, family].set(squares[family])
    blocks = blocks.reshape(LEVELS, heads, LEVELS)
    top = blocks.astype(half)
    low = (blocks - top.astype(single)).astype(half)
    ones = (lax.broadcasted_iota(jnp.int32, (LEVELS, heads, 1), 0) < BINS).astype(half)
    spare = jnp.zeros((LEVELS, heads, LANES - 2 * LEVELS - 1), half)
    columns = jnp.concatenate([top, low, ones, spare], -1).reshape(LEVELS, heads * LANES)
    return jnp.pad(columns, ((0, LANES - LEVELS), (0, 0)))


def key_columns(bins, key_valid):
    tokens = bins.shape[1]
    level = lax.broadcasted_iota(jnp.int32, (tokens, BINS), 1)
    onehot = jnp.concatenate([(bins[f][:, None] == level).astype(half) for f in range(3)], -1)
    masked = jnp.where(key_valid > 0, 0.0, masked_score).astype(half)[:, None]
    spare = jnp.zeros((tokens, LANES - 2 * LEVELS - 1), half)
    return jnp.concatenate([onehot, onehot, masked, spare], -1)


def relative_grad(sums, offsets):
    pairs = sums.shape[0]
    sums = sums.reshape(pairs * PAIR, LEVELS, LANES)[:, :, :LEVELS]
    pieces = []
    for family in range(3):
        part = slice(family * BINS, (family + 1) * BINS)
        pieces.append(jnp.einsum("hca,acr->hr", sums[:, part, part], offsets, precision=highest))
    return jnp.concatenate(pieces, -1)


def body(
    features,
    box_bins,
    text_mask,
    spatial_table,
    joint_projection,
    spatial_projection,
    relative_table,
    output_projection,
    output_bias,
    norm_one_gain,
    norm_one_shift,
    up_weight,
    up_bias,
    down_weight,
    down_bias,
    norm_two_gain,
    norm_two_shift,
    output_cotangent,
    *,
    count,
):
    tokens, width = features.shape[1:]
    heads = relative_table.shape[1]
    table_rows = spatial_table.shape[0]
    page_count = tokens // SLOTS
    stream_side = lax.axis_index("stream")
    key_valid = jnp.where(stream_side == 0, text_mask, jnp.ones_like(text_mask))
    inputs = features[0]
    bins = box_bins[0]
    gain_one, shift_one = norm_one_gain[0], norm_one_shift[0]
    gain_two, shift_two = norm_two_gain[0], norm_two_shift[0]

    early = jnp.concatenate([joint_projection, spatial_projection, output_projection], -1)
    early = lax.all_gather(early, "pages", axis=1, tiled=True)[0]
    full_joint = early[:, : 3 * width]
    full_spatial = early[:, 3 * width : 5 * width]
    full_output = early[:, 5 * width :]
    full_up = lax.all_gather(up_weight, "pages", axis=1, tiled=True)[0]
    full_down = lax.all_gather(down_weight, "pages", axis=1, tiled=True)[0]

    offsets = level_offsets()
    rel = relative_columns(relative_table[0], offsets)
    keyx = key_columns(bins, key_valid)
    cell_ids = bins[2] * BINS + bins[1]
    cells = (cell_ids[:, None] == lax.broadcasted_iota(jnp.int32, (tokens, table_rows), 1)).astype(half)
    cells_t = (cell_ids[None, :] == lax.broadcasted_iota(jnp.int32, (table_rows, tokens), 0)).astype(half)

    joint_half = times(inputs, full_joint).astype(half)
    spatial_rows = times(spatial_table, full_spatial).astype(half)
    mixtures, logs, joined = [], [], []
    for page in range(page_count):
        mixture, own, sent, log_total = attend_page(
            page, joint_half, spatial_rows, cells, keyx, rel, full_output, output_bias, heads
        )
        mixtures.append(mixture)
        logs.append(log_total)
        joined.append(own + swap_streams(sent).astype(single))
    mixture = jnp.concatenate(mixtures, 0)
    joined = jnp.concatenate(joined, 0)

    normed_one, inverse_one = layer_stats(inputs.astype(single) + joined)
    hidden = normed_one * gain_one + shift_one
    hidden_half = hidden.astype(half)
    activated, slope = gelu_slope(times(hidden_half, full_up) + up_bias[0])
    active_half = activated.astype(half)
    normed_two, inverse_two = layer_stats(hidden + (times(active_half, full_down) + down_bias[0]))
    layer_output = (normed_two * gain_two + shift_two).astype(half)
    upstream = output_cotangent[0].astype(single)
    grad_resid_two = norm_back(upstream * gain_two, normed_two, inverse_two)
    grad_branch = grad_resid_two.astype(half)
    grad_down = summed_rows(active_half, grad_branch, count, width, by_rows=True)
    grad_pre = (times_transposed(grad_branch, full_down) * slope).astype(half)
    grad_hidden = grad_resid_two + times_transposed(grad_pre, full_up)
    grad_resid_one = norm_back(grad_hidden * gain_one, normed_one, inverse_one)
    grad_up = summed_rows(hidden_half, grad_pre, count, width)

    grad_attention, before = [], None
    for page in range(page_count):
        part = grad_resid_one[page * SLOTS : (page + 1) * SLOTS]
        part = (part + swap_streams(part.astype(half)).astype(single)).astype(half)
        grad_attention.append(part)
        before = attend_page_back(
            page, joint_half, spatial_rows, cells, cells_t, keyx, rel, logs[page], part, full_output,
            heads, before,
        )
    grad_rows, cell_q, cell_k, bin_sums = before
    grad_attention = jnp.concatenate(grad_attention, 0)
    grad_output = summed_rows(mixture, grad_attention, count, width)
    grad_joint = summed_rows(inputs, grad_rows, count, width)
    cell_half = jnp.concatenate([cell_q, cell_k], 1).astype(half)
    grad_spatial = summed_rows(spatial_table, cell_half, count, width)
    grad_table = sum_pages(times_transposed(cell_half, full_spatial), count, half)
    grad_table = rounded(grad_table, half)
    grad_table = grad_table + swap_streams(grad_table.astype(half)).astype(single)
    grad_features = input_grad(grad_rows, full_joint, grad_resid_one)

    small = [
        jnp.sum(grad_hidden * normed_one, 0),
        jnp.sum(grad_hidden, 0),
        jnp.sum(grad_attention.astype(single), 0),
        jnp.sum(grad_pre.astype(single), 0),
        jnp.sum(grad_branch.astype(single), 0),
        jnp.sum(upstream * normed_two, 0),
        jnp.sum(upstream, 0),
        relative_grad(bin_sums, offsets).reshape(-1),
    ]
    ends = []
    for piece in small:
        ends.append((ends[-1] if ends else 0) + piece.shape[0])
    packed = jnp.concatenate(small)
    packed = jnp.pad(packed, (0, -ends[-1] % (8 * LANES))).reshape(-1, LANES)
    packed = sum_pages(packed, count, single).reshape(-1)
    small = [packed[end - piece.shape[0] : end] for end, piece in zip(ends, small)]

    return (
        layer_output[None],
        grad_features[None],
        grad_joint,
        grad_spatial,
        small[7].reshape(relative_table.shape),
        grad_output,
        small[2][None],
        small[0][None],
        small[1][None],
        grad_up,
        small[3][None],
        grad_down,
        small[4][None],
        small[5][None],
        small[6][None],
        grad_table,
    )


def solution(mesh):
    rows = P("stream", "pages", None)
    vector = P("stream", None)
    placed = (
        rows,
        P("stream", None, "pages"),
        P("pages"),
        P(),
        rows,
        rows,
        P("stream", None, None),
        rows,
        vector,
        vector,
        vector,
        rows,
        vector,
        rows,
        vector,
        vector,
        vector,
        rows,
    )
    out_specs = (
        rows,
        rows,
        rows,
        rows,
        P("stream", None, None),
        rows,
        vector,
        vector,
        vector,
        rows,
        vector,
        rows,
        vector,
        vector,
        vector,
        P(),
    )
    return jax.shard_map(
        functools.partial(body, count=mesh.shape["pages"]),
        mesh=mesh,
        in_specs=placed,
        out_specs=out_specs,
        check_vma=False,
    )
```

time: 1250 us -> 562 us (0.45)
  waiting for transfers between devices: 720 us -> 217 us
  blocking collectives: 138 us -> 0 us
  matrix products: 201 us -> 66 us
  Pallas kernels: 0 us -> 101 us
  local copies, waits for them, and re-layouts: 107 us -> 53.9 us
  starting transfers between devices: 1.09 us -> 41.1 us
    reduce_scatter x3 -> x0, waiting for transfers between devices: 294 us -> none  [the longest x1 116 us: body(): lax.psum_scatter(local_grads[3][None], 'pages', scatter_dimension=1, tile...]
    unnamed x12 -> x3, waiting for transfers between devices: 196 us -> 1.39 us
    psum x2 -> x0, blocking collectives: 138 us -> none  [the longest x1 78 us: body(): grad_joined = lax.psum(grad_resid_one, 'stream')]
    dot_general x53 -> x11, matrix products: 199 us -> 66 us  [the longest x4 31.5 us: times(): return jnp.dot(left, right, preferred_element_type=single)]
    ppermute x0 -> x38, waiting for transfers between devices: none -> 131 us  [the longest x5 59.9 us: scatter_sum(): received_x = lax.ppermute(send, 'pages', flip(count, 2))]
    pallas_call x0 -> x10, Pallas kernels: none -> 101 us  [the longest x2 35.7 us: attend_page_back(): pl.pallas_call(functools.partial(backward_kernel, scale=size ** (-0.5), s...]
    psum x2 -> x0, waiting for transfers between devices: 79.4 us -> none  [the longest x1 79.4 us: body(): joined = lax.psum(attention_out, 'stream')]
    all_gather x5 -> x3, waiting for transfers between devices: 150 us -> 84.9 us  [the longest x1 58.3 us: body(): early = lax.all_gather(early, 'pages', axis=1, tiled=True)[0]]
  transfers between devices with their start and end apart: 11 -> 41, of which waited for: 9 -> 20; matrix products, arithmetic and copies ran while one was open for 13% -> 19% of each run, Pallas kernels for 0% -> 18%
where the time goes in v1:
time: 562 us; the launch traced here: 552 us
  waiting for transfers between devices  217 us (39%)
  Pallas kernels  101 us (18%)
  matrix products  66 us (12%)
  other arithmetic  58.2 us (10%)
  local copies, waits for them, and re-layouts  53.9 us (10%)
  starting transfers between devices  41.1 us (7%)
  between operations  15.1 us (3%)
    ppermute x5, waiting for transfers between devices, scatter_sum(): received_x = lax.ppermute(send, 'pages', flip(count, 2))  59.9 us
    all_gather x1, waiting for transfers between devices, body(): early = lax.all_gather(early, 'pages', axis=1, tiled=True)[0]  58.3 us
    ppermute x15, waiting for transfers between devices, scatter_sum(): lax.ppermute(part, 'pages', flip(count, 4 * slot)).astype(single)  49.8 us
    unnamed x149, local copies, waits for them, and re-layouts  36.8 us
    pallas_call x2, Pallas kernels, attend_page_back(): pl.pallas_call(functools.partial(backward_kernel, scale=size ** (-0.5), s...  35.7 us
    dot_general x4, matrix products, times(): return jnp.dot(left, right, preferred_element_type=single)  31.5 us
    dot_general x3, matrix products, times_transposed(): lax.dot_general(left, right, (((1,), (1,)), ((), ())), preferred_element_...  30.7 us
    pallas_call x5, Pallas kernels, weight_grads(): pl.pallas_call(functools.partial(grads_kernel, blocks=blocks, by_rows=by_...  30.6 us
  transfers between devices with their start and end apart: 41, of which 20 were waited for; matrix products, arithmetic and copies ran while one was open for 19% of the time, Pallas kernels for 18%

profile of v1, /device:TPU:8, one launch (start us, length us, event | category | flops | bytes accessed | tf_op | source)
XLA Modules:
  0.0 552.0 jit_solution(17747443649009282948)
XLA Ops:
  7.2 1.8 pad_maximum_fusion.3
  12.8 1.8 copy.48
  16.0 3.6 concatenate.44.keyx_ref
  19.9 58.3 %all-gather.4.cloned.1.call-done = bf16[1,768,4608]{2,1,0:T(8,128)(2,1)} async-done(((bf16[1,48,4608]{2,1,0:T(8,128)(2,1)}), bf16[1,768,4608]{2,1,0:T(8,128)(2,1)}) %all-gather.4.cloned.1.call-update) | async-done | bytes 7077904 | tf_op jit(solution)/shard_map/all_gather | solution.py:492
  79.6 2.9 fusion.29.sq_ref.sk_ref
  82.5 6.3 %fusion.6.q_ref.k_ref.v_ref = bf16[1024,2304]{1,0:T(8,128)(2,1)S(1)} fusion(bf16[1,1024,768]{2,1,0:T(8,128)(2,1)S(1)} %copy-done.19, bf16[768,4608]{1,0:T(8,128)(2,1)} %bitcast.247), kind=kOutput, calls=%fused_computation.11 | convolution fusion | flops 3626237952 | bytes 9830400 | tf_op jit(solution)/shard_map/dot_general | solution.py:25
  88.9 13.7 %attend_page.2 = (bf16[512,768]{1,0:T(8,128)(2,1)S(1)}, f32[512,768]{1,0:T(8,128)S(1)}, bf16[512,768]{1,0:T(8,128)(2,1)}, f32[12,512]{1,0:T(8,128)S(1)}) custom-call(bf16[1024,2304]{1,0:T(8,128)(2,1)S(1)} %fusion.6.q_ref.k_ref.v_ref, bf16[1024,2304]{1,0:T(8,128)(2,1)S(1)} %fusion.6.q_ref.k_ref.v_ref, bf16[1024,2304]{1,0:T(8,128)(2,1)S(1)} %fusion.6.q_ref.k_ref.v_ref, ...), custom_call_target="tpu_custom_call" | custom-call | flops 2415919104 | bytes 4718592 | tf_op jit(solution)/shard_map/attend_page/pallas_call | solution.py:237
  104.3 1.5 collective-permute-start
  105.8 13.7 %attend_page.3 = (bf16[512,768]{1,0:T(8,128)(2,1)S(1)}, f32[512,768]{1,0:T(8,128)S(1)}, bf16[512,768]{1,0:T(8,128)(2,1)}, f32[12,512]{1,0:T(8,128)S(1)}) custom-call(bf16[1024,2304]{1,0:T(8,128)(2,1)S(1)} %fusion.6.q_ref.k_ref.v_ref, bf16[1024,2304]{1,0:T(8,128)(2,1)S(1)} %fusion.6.q_ref.k_ref.v_ref, bf16[1024,2304]{1,0:T(8,128)(2,1)S(1)} %fusion.6.q_ref.k_ref.v_ref, ...), custom_call_target="tpu_custom_call" | custom-call | flops 2415919104 | bytes 4718592 | tf_op jit(solution)/shard_map/attend_page/pallas_call | solution.py:237
  128.3 4.1 slice.439.weight_ref
  135.8 6.1 %collective-permute-done.1 = bf16[512,768]{1,0:T(8,128)(2,1)} collective-permute-done((bf16[512,768]{1,0:T(8,128)(2,1)}, bf16[512,768]{1,0:T(8,128)(2,1)}, u32[]{:S(2)}, u32[]{:S(2)}) %collective-permute-start.1) | collective-permute-done | bytes 786464 | tf_op jit(solution)/shard_map/ppermute | solution.py:61
  144.4 1.7 copy-done.40
  146.6 13.0 %multiply_convert_fusion = (bf16[1024,3072]{1,0:T(8,128)(2,1)}, f32[1024,3072]{1,0:T(8,128)}) fusion(f32[3072]{0:T(1024)} %bitcast.265, bf16[1,768,3072]{2,1,0:T(8,128)(2,1)} %all-gather.6.cloned.1.call-done, f32[1,512,768]{2,1,0:T(8,128)} %bitcast.243, f32[1,512,768]{2,1,0:T(8,128)S(1)} %bitcast.242, bf16[1,1024,768]{2,1,0:T(8,128)(2,1)S(1)} %copy-done.19, ...), kind=kOutput, calls=%fused_computation.8 | convolution fusion | flops 4857004032 | bytes 28338176 | tf_op jit(solution)/shard_map/dot_general | solution.py:25
  159.7 26.6 %all-gather.8.cloned.1.call-done = bf16[1,3072,768]{2,1,0:T(8,128)(2,1)} async-done(((bf16[1,192,768]{2,1,0:T(8,128)(2,1)}), bf16[1,3072,768]{2,1,0:T(8,128)(2,1)}) %all-gather.8.cloned.1.call-update) | async-done | bytes 4718608 | tf_op jit(solution)/shard_map/all_gather | solution.py:497
  186.3 9.3 %fusion.106 = (f32[1024]{0:T(1024)S(1)}, f32[1024,768]{1,0:T(8,128)S(1)}) fusion(f32[768]{0:T(1024)} %reduce.10, bf16[1024,3072]{1,0:T(8,128)(2,1)} %get-tuple-element.162.lhs_ref, bf16[1,3072,768]{2,1,0:T(8,128)(2,1)} %all-gather.8.cloned.1.call-done, f32[768]{0:T(1024)} %reduce.9, f32[768]{0:T(1024)S(1)} %reduce.8, f32[1024]{0:T(1024)S(1)} %add_rsqrt_fusion.1, ...), kind=kOutput, calls=%fused_computation.216 | convolution fusion | flops 4837342208 | bytes 17323008 | tf_op jit(solution)/shard_map/dot_general | solution.py:25
  196.2 2.0 copy-done.44
  198.2 1.9 fusion.22
  200.1 3.0 convert_reduce_fusion.2
  203.1 12.4 %convert_reduce_fusion = (f32[3072]{0:T(1024)}, bf16[1024,3072]{1,0:T(8,128)(2,1)S(1)}) fusion(f32[1024,3072]{1,0:T(8,128)} %get-tuple-element.163, f32[3072]{0:T(1024)S(1)} %bitcast.266, bf16[1024,768]{1,0:T(8,128)(2,1)S(1)} %get-tuple-element.114.rhs_ref, bf16[1,3072,768]{2,1,0:T(8,128)(2,1)S(1)} %bitcast.264), kind=kOutput, calls=%fused_computation.7 | convolution fusion | flops 4872729600 | bytes 25190400 | tf_op jit(solution)/shard_map/dot_general | solution.py:33
  215.5 13.1 %multiply_reduce_fusion = (f32[768]{0:T(1024)S(1)}, f32[1024]{0:T(1024)S(1)}, f32[1024]{0:T(1024)S(1)}, f32[768]{0:T(1024)S(1)}, bf16[1024,768]{1,0:T(8,128)(2,1)S(1)}, /*index=5*/f32[1024,768]{1,0:T(8,128)}) fusion(f32[1024,768]{1,0:T(8,128)S(1)} %copy-done.41, f32[1024]{0:T(1024)S(1)} %add_rsqrt_fusion.1, f32[1024]{0:T(1024)S(1)} %broadcast_multiply_fusion.5, ...), kind=kOutput, calls=%fused_computation.39 | convolution fusion | flops 4848349184 | bytes 23641088 | tf_op jit(solution)/shard_map/dot_general | solution.py:33
  228.6 13.1 %subtract_multiply_fusion.resid_ref = f32[1024,768]{1,0:T(8,128)S(1)} fusion(f32[1024,768]{1,0:T(8,128)} %get-tuple-element.166, f32[1024,768]{1,0:T(8,128)} %copy-done.40, f32[1024]{0:T(1024)S(1)} %broadcast_multiply_fusion, f32[1024]{0:T(1024)S(1)} %broadcast_multiply_fusion.1, f32[768]{0:T(1024)S(1)} %reduce.8, f32[1024]{0:T(1024)S(1)} %add_rsqrt_fusion.1, ...), kind=kLoop, calls=%fused_computation.40 | loop fusion | flops 5505024 | bytes 9456640 | tf_op jit(solution)/shard_map/mul | solution.py:43
  241.9 1.5 collective-permute-start.2
  244.0 8.6 %weight_grads.9 = (bf16[8,192,768]{2,1,0:T(8,128)(2,1)S(1)}, bf16[8,192,768]{2,1,0:T(8,128)(2,1)}) custom-call(bf16[1024,3072]{1,0:T(8,128)(2,1)S(1)} %bitcast.241, bf16[1024,768]{1,0:T(8,128)(2,1)S(1)} %get-tuple-element.114.rhs_ref), custom_call_target="tpu_custom_call" | custom-call | flops 4831838208 | bytes 12582912 | tf_op jit(solution)/shard_map/weight_grads/pallas_call | solution.py:142
  254.0 2.8 copy-done.39
  256.8 9.2 %weight_grads.8 = (bf16[8,48,3072]{2,1,0:T(8,128)(2,1)S(1)}, bf16[8,48,3072]{2,1,0:T(8,128)(2,1)}) custom-call(bf16[1024,768]{1,0:T(8,128)(2,1)S(1)} %get-tuple-element.125.lhs_ref, bf16[1024,3072]{1,0:T(8,128)(2,1)S(1)} %copy-done.39), custom_call_target="tpu_custom_call" | custom-call | flops 4831838208 | bytes 12582912 | tf_op jit(solution)/shard_map/weight_grads/pallas_call | solution.py:142
  269.2 9.3 %collective-permute-done.3 = bf16[512,768]{1,0:T(8,128)(2,1)S(1)} collective-permute-done((bf16[512,768]{1,0:T(8,128)(2,1)S(1)}, bf16[512,768]{1,0:T(8,128)(2,1)S(1)}, u32[]{:S(2)}, u32[]{:S(2)}) %collective-permute-start.3) | collective-permute-done | bytes 786464 | tf_op jit(solution)/shard_map/ppermute | solution.py:61
  280.7 17.9 %attend_page_back.2 = (bf16[3,1024,768]{2,1,0:T(8,128)(2,1)S(1)}, f32[256,768]{1,0:T(8,128)S(1)}, f32[256,768]{1,0:T(8,128)S(1)}, f32[6,96,128]{2,1,0:T(8,128)S(1)}) custom-call(bf16[1024,2304]{1,0:T(8,128)(2,1)S(1)} %bitcast.237, bf16[1024,2304]{1,0:T(8,128)(2,1)S(1)} %bitcast.237, bf16[1024,2304]{1,0:T(8,128)(2,1)S(1)} %bitcast.237, ...), custom_call_target="tpu_custom_call" | custom-call | flops 6442450944 | bytes 7864320 | tf_op jit(solution)/shard_map/attend_page_back/pallas_call | solution.py:341
  298.6 17.9 %attend_page_back.3 = (bf16[3,1024,768]{2,1,0:T(8,128)(2,1)S(1)}, f32[256,768]{1,0:T(8,128)S(1)}, f32[256,768]{1,0:T(8,128)S(1)}, f32[6,96,128]{2,1,0:T(8,128)S(1)}) custom-call(bf16[1024,2304]{1,0:T(8,128)(2,1)S(1)} %bitcast.237, bf16[1024,2304]{1,0:T(8,128)(2,1)S(1)} %bitcast.237, ...), custom_call_target="tpu_custom_call", output_to_operand_aliasing={{0}: (12, {}), {1}: (13, {}), {2}: (14, {}), {3}: (15, {})} | custom-call | flops 6442450944 | bytes 7864320 | tf_op jit(solution)/shard_map/attend_page_back/pallas_call | solution.py:341
  316.6 5.2 fusion.107
  321.9 3.2 weight_grads.7
  326.4 1.6 copy.58
  329.2 1.7 copy.57
  332.0 1.7 copy.56
  345.1 2.3 copy-done.6
  348.9 6.9 %weight_grads.5 = (bf16[8,48,2304]{2,1,0:T(8,128)(2,1)S(1)}, bf16[8,48,2304]{2,1,0:T(8,128)(2,1)S(1)}) custom-call(bf16[1024,768]{1,0:T(8,128)(2,1)S(1)} %bitcast.238, bf16[3,1024,768]{2,1,0:T(8,128)(2,1)S(1)} %copy-done.6), custom_call_target="tpu_custom_call" | custom-call | flops 3623878656 | bytes 9830400 | tf_op jit(solution)/shard_map/weight_grads/pallas_call | solution.py:142
  356.5 7.1 %input_grad.1 = f32[1024,768]{1,0:T(8,128)} custom-call(bf16[3,1024,768]{2,1,0:T(8,128)(2,1)S(1)} %copy-done.6, bf16[768,2304]{1,0:T(8,128)(2,1)S(1)} %copy-done.7, f32[1024,768]{1,0:T(8,128)S(1)} %subtract_multiply_fusion.resid_ref), custom_call_target="tpu_custom_call" | custom-call | flops 3623878656 | bytes 11010048 | tf_op jit(solution)/shard_map/input_grad/pallas_call | solution.py:396
  365.3 1.5 collective-permute-start.34
  368.7 1.9 collective-permute-start.17
  370.6 2.7 weight_grads.6
  373.7 8.8 %collective-permute-done.19 = bf16[4,48,768]{2,1,0:T(8,128)(2,1)S(1)} collective-permute-done((bf16[4,48,768]{2,1,0:T(8,128)(2,1)S(1)}, bf16[4,48,768]{2,1,0:T(8,128)(2,1)S(1)}, u32[]{:S(2)}, u32[]{:S(2)}) %collective-permute-start.19) | collective-permute-done | bytes 294944 | tf_op jit(solution)/shard_map/ppermute | solution.py:170
  383.3 1.5 collective-permute-start.20
  385.7 2.2 fusion.100
  395.9 1.7 fusion.82
  400.4 5.0 collective-permute-start.36
  405.3 1.5 add_convert_fusion.10
  406.9 1.5 collective-permute-start.10
  408.4 2.3 add_convert_fusion.2
  411.4 2.7 add_convert_fusion.4
  414.1 9.1 %collective-permute-done.10 = bf16[4,48,1536]{2,1,0:T(8,128)(2,1)S(1)} collective-permute-done((bf16[4,48,1536]{2,1,0:T(8,128)(2,1)S(1)}, bf16[4,48,1536]{2,1,0:T(8,128)(2,1)S(1)}, u32[]{:S(2)}, u32[]{:S(2)}) %collective-permute-start.10) | collective-permute-done | bytes 589856 | tf_op jit(solution)/shard_map/ppermute | solution.py:170
  423.3 2.5 collective-permute-start.12
  427.2 1.5 collective-permute-start.5
  431.5 3.6 collective-permute-done.12
  435.1 1.5 collective-permute-start.37
  436.6 1.8 collective-permute-done.13
  439.2 3.7 collective-permute-done.37
  442.9 2.1 convert_add_fusion.2
  445.0 22.4 %collective-permute-done.5 = bf16[4,48,2304]{2,1,0:T(8,128)(2,1)S(1)} collective-permute-done((bf16[4,48,2304]{2,1,0:T(8,128)(2,1)S(1)}, bf16[4,48,2304]{2,1,0:T(8,128)(2,1)S(1)}, u32[]{:S(2)}, u32[]{:S(2)}) %collective-permute-start.5) | collective-permute-done | bytes 884768 | tf_op jit(solution)/shard_map/ppermute | solution.py:170
  467.6 2.5 collective-permute-start.7
  472.4 19.6 %collective-permute-done.24 = bf16[4,48,3072]{2,1,0:T(8,128)(2,1)S(1)} collective-permute-done((bf16[4,48,3072]{2,1,0:T(8,128)(2,1)S(1)}, bf16[4,48,3072]{2,1,0:T(8,128)(2,1)S(1)}, u32[]{:S(2)}, u32[]{:S(2)}) %collective-permute-start.24) | collective-permute-done | bytes 1179680 | tf_op jit(solution)/shard_map/ppermute | solution.py:170
  493.6 3.0 collective-permute-start.25
  499.0 14.2 %collective-permute-done.31 = bf16[192,768]{1,0:T(8,128)(2,1)S(1)} collective-permute-done((bf16[192,768]{1,0:T(8,128)(2,1)S(1)}, bf16[192,768]{1,0:T(8,128)(2,1)S(1)}, u32[]{:S(2)}, u32[]{:S(2)}) %collective-permute-start.31) | collective-permute-done | bytes 294944 | tf_op jit(solution)/shard_map/ppermute | solution.py:175
  513.3 19.5 %collective-permute-done.32 = bf16[192,768]{1,0:T(8,128)(2,1)S(1)} collective-permute-done((bf16[192,768]{1,0:T(8,128)(2,1)S(1)}, bf16[192,768]{1,0:T(8,128)(2,1)S(1)}, u32[]{:S(2)}, u32[]{:S(2)}) %collective-permute-start.32) | collective-permute-done | bytes 294944 | tf_op jit(solution)/shard_map/ppermute | solution.py:175
  533.7 3.8 collective-permute-done.26
  537.6 6.5 %collective-permute-done.27 = bf16[48,3072]{1,0:T(8,128)(2,1)S(1)} collective-permute-done((bf16[48,3072]{1,0:T(8,128)(2,1)S(1)}, bf16[48,3072]{1,0:T(8,128)(2,1)S(1)}, u32[]{:S(2)}, u32[]{:S(2)}) %collective-permute-start.27) | collective-permute-done | bytes 294944 | tf_op jit(solution)/shard_map/ppermute | solution.py:175
  (285 shorter events, 79.6 us)
Async XLA Ops:
  7.2 70.9 %all-gather.4.cloned.1.call-start = ((), (), s32[]{:S(2)}) async-start(), calls=%async_computation | async-start | bytes 7520256 | tf_op jit(solution)/shard_map/all_gather | solution.py:492
  9.1 137.5 %all-gather.6.cloned.1.call-start = ((), (), s32[]{:S(2)}) async-start(), calls=%async_computation.1 | async-start | bytes 5013504 | tf_op jit(solution)/shard_map/all_gather | solution.py:496
  9.8 176.5 %all-gather.8.cloned.1.call-start = ((), (), s32[]{:S(2)}) async-start(), calls=%async_computation.2 | async-start | bytes 5013504 | tf_op jit(solution)/shard_map/all_gather | solution.py:497
  15.4 64.2 %copy-start.34 = (bf16[256,768]{1,0:T(8,128)(2,1)S(1)}, bf16[256,768]{1,0:T(8,128)(2,1)}, u32[]{:S(2)}) copy-start(bf16[256,768]{1,0:T(8,128)(2,1)} %lhs_ref.1) | copy-start | bytes 1179652
  19.6 86.2 %copy-start.10 = (bf16[1024,128]{1,0:T(8,128)(2,1)}, bf16[1024,128]{1,0:T(8,128)(2,1)S(1)}, u32[]{:S(2)}) copy-start(bf16[1024,128]{1,0:T(8,128)(2,1)S(1)} %concatenate.44.keyx_ref) | copy-start | bytes 786436
  19.8 85.9 %copy-start.8 = (bf16[1024,256]{1,0:T(8,128)(2,1)}, bf16[1024,256]{1,0:T(8,128)(2,1)S(1)}, u32[]{:S(2)}) copy-start(bf16[1024,256]{1,0:T(8,128)(2,1)S(1)} %fusion.48.cells_ref) | copy-start | bytes 1572868
  79.6 26.2 %copy-start.3 = (bf16[768,768]{1,0:T(8,128)(2,1)}, bf16[768,768]{1,0:T(8,128)(2,1)S(1)}, u32[]{:S(2)}) copy-start(bf16[768,768]{1,0:T(8,128)(2,1)S(1)} %slice.444.out_w_ref) | copy-start | bytes 3538948
  82.5 23.3 %copy-start.1 = (bf16[256,1536]{1,0:T(8,128)(2,1)}, bf16[256,1536]{1,0:T(8,128)(2,1)S(1)}, u32[]{:S(2)}) copy-start(bf16[256,1536]{1,0:T(8,128)(2,1)S(1)} %fusion.29.sq_ref.sk_ref) | copy-start | bytes 2359300
  88.8 16.9 %copy-start = (bf16[1024,2304]{1,0:T(8,128)(2,1)}, bf16[1024,2304]{1,0:T(8,128)(2,1)S(1)}, u32[]{:S(2)}) copy-start(bf16[1024,2304]{1,0:T(8,128)(2,1)S(1)} %fusion.6.q_ref.k_ref.v_ref) | copy-start | bytes 14155780
  104.3 18.4 %copy-start.43 = (bf16[1,1024,768]{2,1,0:T(8,128)(2,1)S(1)}, bf16[1,1024,768]{2,1,0:T(8,128)(2,1)}, u32[]{:S(2)}) copy-start(bf16[1,1024,768]{2,1,0:T(8,128)(2,1)} %param.41) | copy-start | bytes 4718596
  104.3 19.2 %copy-start.57 = (f32[1,768]{1,0:T(1,128)S(1)}, f32[1,768]{1,0:T(1,128)}, u32[]{:S(2)}) copy-start(f32[1,768]{1,0:T(1,128)} %param.33) | copy-start | bytes 9220
  104.3 19.2 %copy-start.58 = (f32[1,768]{1,0:T(1,128)S(1)}, f32[1,768]{1,0:T(1,128)}, u32[]{:S(2)}) copy-start(f32[1,768]{1,0:T(1,128)} %param.34) | copy-start | bytes 9220
  104.3 29.4 %collective-permute-start = (bf16[512,768]{1,0:T(8,128)(2,1)}, bf16[512,768]{1,0:T(8,128)(2,1)}, u32[]{:S(2)}, u32[]{:S(2)}) collective-permute-start(bf16[512,768]{1,0:T(8,128)(2,1)} %get-tuple-element.79), channel_id=1, source_target_pairs={{0,16},{16,0},{1,17},{17,1},{2,18},{18,2},{3,19},{19,3},{4,20},{20... | collective-permute-start | bytes 2359304 | tf_op jit(solution)/shard_map/ppermute | solution.py:61
  122.1 19.7 %collective-permute-start.1 = (bf16[512,768]{1,0:T(8,128)(2,1)}, bf16[512,768]{1,0:T(8,128)(2,1)}, u32[]{:S(2)}, u32[]{:S(2)}) collective-permute-start(bf16[512,768]{1,0:T(8,128)(2,1)} %get-tuple-element.81), channel_id=1, source_target_pairs={{0,16},{16,0},{1,17},{17,1},{2,18},{18,2},{3,19},{19,3},{4,20},{20... | collective-permute-start | bytes 2359304 | tf_op jit(solution)/shard_map/ppermute | solution.py:61
  132.4 9.4 %copy-start.25 = (f32[512,768]{1,0:T(8,128)S(1)}, f32[512,768]{1,0:T(8,128)}, u32[]{:S(2)}) copy-start(f32[512,768]{1,0:T(8,128)} %copy-done.24) | copy-start | bytes 4718596
  203.1 12.4 %copy-start.41 = (f32[1024,768]{1,0:T(8,128)S(1)}, f32[1024,768]{1,0:T(8,128)}, u32[]{:S(2)}) copy-start(f32[1024,768]{1,0:T(8,128)} %copy-done.40) | copy-start | bytes 9437188
  203.1 12.4 %copy-start.56 = (f32[768]{0:T(1024)S(1)}, f32[768]{0:T(1024)}, u32[]{:S(2)}) copy-start(f32[768]{0:T(1024)} %reduce.9) | copy-start | bytes 9220
  203.1 40.9 %slice-start.2 = ((s8[6291456]{0:T(1024)(128)(4,1)}), s8[4194304]{0:T(1024)(128)(4,1)S(1)}, s32[]{:S(2)}) async-start(s8[6291456]{0:T(1024)(128)(4,1)} %bitcast.240), calls=%async_computation.5 | async-start | bytes 8388608
  215.5 13.1 %copy-start.38 = (bf16[1024,3072]{1,0:T(8,128)(2,1)}, bf16[1024,3072]{1,0:T(8,128)(2,1)S(1)}, u32[]{:S(2)}) copy-start(bf16[1024,3072]{1,0:T(8,128)(2,1)S(1)} %get-tuple-element.168.rhs_ref) | copy-start | bytes 18874372
  215.5 28.5 %slice-start.3 = ((s8[6291456]{0:T(1024)(128)(4,1)}), s8[2097152]{0:T(1024)(128)(4,1)S(1)}, s32[]{:S(2)}) async-start(s8[6291456]{0:T(1024)(128)(4,1)} %bitcast.240), calls=%async_computation.6 | async-start | bytes 4194304
  241.9 27.3 %collective-permute-start.2 = (bf16[512,768]{1,0:T(8,128)(2,1)S(1)}, bf16[512,768]{1,0:T(8,128)(2,1)S(1)}, u32[]{:S(2)}, u32[]{:S(2)}) collective-permute-start(bf16[512,768]{1,0:T(8,128)(2,1)S(1)} %get-tuple-element.130), channel_id=1, source_target_pairs={{0,16},{16,0},{1,17},{17,1},{2,18},{18,2},{3,19},{19,3},{4,20},{20... | collective-permute-start | bytes 2359304 | tf_op jit(solution)/shard_map/ppermute | solution.py:61
  243.4 35.1 %collective-permute-start.3 = (bf16[512,768]{1,0:T(8,128)(2,1)S(1)}, bf16[512,768]{1,0:T(8,128)(2,1)S(1)}, u32[]{:S(2)}, u32[]{:S(2)}) collective-permute-start(bf16[512,768]{1,0:T(8,128)(2,1)S(1)} %get-tuple-element.129), channel_id=1, source_target_pairs={{0,16},{16,0},{1,17},{17,1},{2,18},{18,2},{3,19},{19,3},{4,20},{20... | collective-permute-start | bytes 2359304 | tf_op jit(solution)/shard_map/ppermute | solution.py:61
  244.0 35.9 %slice-start = ((s8[4718592]{0:T(1024)(128)(4,1)}), s8[4194304]{0:T(1024)(128)(4,1)S(1)}, s32[]{:S(2)}) async-start(s8[4718592]{0:T(1024)(128)(4,1)} %bitcast.236), calls=%async_computation.3 | async-start | bytes 8388608
  254.0 154.4 %collective-permute-start.28 = (bf16[8,192,768]{2,1,0:T(8,128)(2,1)}, bf16[8,192,768]{2,1,0:T(8,128)(2,1)}, u32[]{:S(2)}, u32[]{:S(2)}) collective-permute-start(bf16[8,192,768]{2,1,0:T(8,128)(2,1)} %get-tuple-element.103), channel_id=1, source_target_pairs={{0,1},{1,0},{2,3},{3,2},{4,5},{5,4},{6,7},{7,6},{8,9},{9,8},{10,11... | collective-permute-start | bytes 7077896 | tf_op jit(solution)/shard_map/ppermute | solution.py:163
  256.8 23.1 %slice-start.1 = ((s8[4718592]{0:T(1024)(128)(4,1)}), s8[524288]{0:T(1024)(128)(4,1)S(1)}, s32[]{:S(2)}) async-start(s8[4718592]{0:T(1024)(128)(4,1)} %bitcast.236), calls=%async_computation.4 | async-start | bytes 1048576
  266.0 12.8 %copy-start.12 = (bf16[8,48,3072]{2,1,0:T(8,128)(2,1)}, bf16[8,48,3072]{2,1,0:T(8,128)(2,1)S(1)}, u32[]{:S(2)}) copy-start(bf16[8,48,3072]{2,1,0:T(8,128)(2,1)S(1)} %get-tuple-element.100) | copy-start | bytes 7077892
  266.0 145.4 %collective-permute-start.23 = (bf16[8,48,3072]{2,1,0:T(8,128)(2,1)}, bf16[8,48,3072]{2,1,0:T(8,128)(2,1)}, u32[]{:S(2)}, u32[]{:S(2)}) collective-permute-start(bf16[8,48,3072]{2,1,0:T(8,128)(2,1)} %get-tuple-element.101), channel_id=1, source_target_pairs={{0,1},{1,0},{2,3},{3,2},{4,5},{5,4},{6,7},{7,6},{8,9},{9,8},{10,11... | collective-permute-start | bytes 7077896 | tf_op jit(solution)/shard_map/ppermute | solution.py:163
  280.7 17.9 %copy-start.31 = (f32[12,512]{1,0:T(8,128)S(1)}, f32[12,512]{1,0:T(8,128)}, u32[]{:S(2)}) copy-start(f32[12,512]{1,0:T(8,128)} %copy-done.30) | copy-start | bytes 73732
  321.9 42.4 %collective-permute-start.33 = (bf16[256,768]{1,0:T(8,128)(2,1)}, bf16[256,768]{1,0:T(8,128)(2,1)}, u32[]{:S(2)}, u32[]{:S(2)}) collective-permute-start(bf16[256,768]{1,0:T(8,128)(2,1)} %get-tuple-element.169), channel_id=1, source_target_pairs={{0,1},{1,0},{2,3},{3,2},{4,5},{5,4},{6,7},{7,6},{8,9},{9,8},{10,11... | collective-permute-start | bytes 1179656 | tf_op jit(solution)/shard_map/ppermute | solution.py:75
  325.1 41.7 %collective-permute-start.18 = (bf16[8,48,768]{2,1,0:T(8,128)(2,1)}, bf16[8,48,768]{2,1,0:T(8,128)(2,1)}, u32[]{:S(2)}, u32[]{:S(2)}) collective-permute-start(bf16[8,48,768]{2,1,0:T(8,128)(2,1)} %get-tuple-element.99), channel_id=1, source_target_pairs={{0,1},{1,0},{2,3},{3,2},{4,5},{5,4},{6,7},{7,6},{8,9},{9,8},{10,11... | collective-permute-start | bytes 1769480 | tf_op jit(solution)/shard_map/ppermute | solution.py:163
  345.0 10.8 %collective-permute-start.14 = (f32[72,128]{1,0:T(8,128)S(1)}, f32[72,128]{1,0:T(8,128)S(1)}, u32[]{:S(2)}, u32[]{:S(2)}) collective-permute-start(f32[72,128]{1,0:T(8,128)S(1)} %pad_bitcast_fusion), channel_id=1, source_target_pairs={{0,1},{1,0},{2,3},{3,2},{4,5},{5,4},{6,7},{7,6},{8,9},{9,8},{10,11... | collective-permute-start | bytes 110600 | tf_op jit(solution)/shard_map/ppermute | solution.py:75
  355.8 11.0 %copy-start.29 = (bf16[8,48,768]{2,1,0:T(8,128)(2,1)S(1)}, bf16[8,48,768]{2,1,0:T(8,128)(2,1)}, u32[]{:S(2)}) copy-start(bf16[8,48,768]{2,1,0:T(8,128)(2,1)} %copy-done.28) | copy-start | bytes 1769476
  355.9 7.7 %collective-permute-start.15 = (f32[72,128]{1,0:T(8,128)S(1)}, f32[72,128]{1,0:T(8,128)S(1)}, u32[]{:S(2)}, u32[]{:S(2)}) collective-permute-start(f32[72,128]{1,0:T(8,128)S(1)} %fusion.97), channel_id=1, source_target_pairs={{0,2},{1,3},{2,0},{3,1},{4,6},{5,7},{6,4},{7,5},{8,10},{9,11},{10,... | collective-permute-start | bytes 110600 | tf_op jit(solution)/shard_map/ppermute | solution.py:75
  363.6 5.1 collective-permute-start.16
  365.3 19.5 %collective-permute-start.34 = (bf16[256,768]{1,0:T(8,128)(2,1)S(1)}, bf16[256,768]{1,0:T(8,128)(2,1)S(1)}, u32[]{:S(2)}, u32[]{:S(2)}) collective-permute-start(bf16[256,768]{1,0:T(8,128)(2,1)S(1)} %fusion.59), channel_id=1, source_target_pairs={{0,2},{1,3},{2,0},{3,1},{4,6},{5,7},{6,4},{7,5},{8,10},{9,11},{10,... | collective-permute-start | bytes 1179656 | tf_op jit(solution)/shard_map/ppermute | solution.py:75
  368.0 19.9 %copy-start.50 = (bf16[4,48,768]{2,1,0:T(8,128)(2,1)}, bf16[4,48,768]{2,1,0:T(8,128)(2,1)S(1)}, u32[]{:S(2)}) copy-start(bf16[4,48,768]{2,1,0:T(8,128)(2,1)S(1)} %get-tuple-element.142) | copy-start | bytes 884740
  368.0 14.5 %collective-permute-start.19 = (bf16[4,48,768]{2,1,0:T(8,128)(2,1)S(1)}, bf16[4,48,768]{2,1,0:T(8,128)(2,1)S(1)}, u32[]{:S(2)}, u32[]{:S(2)}) collective-permute-start(bf16[4,48,768]{2,1,0:T(8,128)(2,1)S(1)} %get-tuple-element.143), channel_id=1, source_target_pairs={{0,2},{1,3},{2,0},{3,1},{4,6},{5,7},{6,4},{7,5},{8,10},{9,11},{10,... | collective-permute-start | bytes 884744 | tf_op jit(solution)/shard_map/ppermute | solution.py:170
  368.7 5.0 collective-permute-start.17
  373.7 31.7 %collective-permute-start.9 = (bf16[8,48,1536]{2,1,0:T(8,128)(2,1)}, bf16[8,48,1536]{2,1,0:T(8,128)(2,1)}, u32[]{:S(2)}, u32[]{:S(2)}) collective-permute-start(bf16[8,48,1536]{2,1,0:T(8,128)(2,1)} %get-tuple-element.94), channel_id=1, source_target_pairs={{0,1},{1,0},{2,3},{3,2},{4,5},{5,4},{6,7},{7,6},{8,9},{9,8},{10,11... | collective-permute-start | bytes 3538952 | tf_op jit(solution)/shard_map/ppermute | solution.py:163
  383.3 4.7 collective-permute-start.20
  384.8 5.4 collective-permute-start.21
  387.9 20.5 %copy-start.15 = (bf16[8,192,768]{2,1,0:T(8,128)(2,1)S(1)}, bf16[8,192,768]{2,1,0:T(8,128)(2,1)}, u32[]{:S(2)}) copy-start(bf16[8,192,768]{2,1,0:T(8,128)(2,1)} %copy-done.14) | copy-start | bytes 7077892
  388.6 10.5 %collective-permute-start.35 = (bf16[256,768]{1,0:T(8,128)(2,1)}, bf16[256,768]{1,0:T(8,128)(2,1)}, u32[]{:S(2)}, u32[]{:S(2)}) collective-permute-start(bf16[256,768]{1,0:T(8,128)(2,1)} %get-tuple-element.111), channel_id=1, source_target_pairs={{0,4},{1,5},{2,6},{3,7},{4,0},{5,1},{6,2},{7,3},{8,12},{9,13},{10,... | collective-permute-start | bytes 1179656 | tf_op jit(solution)/shard_map/ppermute | solution.py:75
  390.1 5.7 %collective-permute-start.22 = (bf16[48,768]{1,0:T(8,128)(2,1)}, bf16[48,768]{1,0:T(8,128)(2,1)}, u32[]{:S(2)}, u32[]{:S(2)}) collective-permute-start(bf16[48,768]{1,0:T(8,128)(2,1)} %get-tuple-element.148), channel_id=1, source_target_pairs={{0,12},{1,13},{2,14},{3,15},{4,8},{5,9},{6,10},{7,11},{8,4},{9,5},... | collective-permute-start | bytes 221192 | tf_op jit(solution)/shard_map/ppermute | solution.py:175
  395.9 30.0 %collective-permute-start.4 = (bf16[8,48,2304]{2,1,0:T(8,128)(2,1)}, bf16[8,48,2304]{2,1,0:T(8,128)(2,1)S(1)}, u32[]{:S(2)}, u32[]{:S(2)}) collective-permute-start(bf16[8,48,2304]{2,1,0:T(8,128)(2,1)} %copy-done.33), channel_id=1, source_target_pairs={{0,1},{1,0},{2,3},{3,2},{4,5},{5,4},{6,7},{7,6},{8,9},{9,8},{10,11... | collective-permute-start | bytes 5308424 | tf_op jit(solution)/shard_map/ppermute | solution.py:163
  400.4 26.8 %collective-permute-start.36 = (bf16[256,768]{1,0:T(8,128)(2,1)S(1)}, bf16[256,768]{1,0:T(8,128)(2,1)S(1)}, u32[]{:S(2)}, u32[]{:S(2)}) collective-permute-start(bf16[256,768]{1,0:T(8,128)(2,1)S(1)} %fusion.60), channel_id=1, source_target_pairs={{0,8},{1,9},{2,10},{3,11},{4,12},{5,13},{6,14},{7,15},{8,0},{9,1},... | collective-permute-start | bytes 1179656 | tf_op jit(solution)/shard_map/ppermute | solution.py:75
  406.9 16.3 %collective-permute-start.10 = (bf16[4,48,1536]{2,1,0:T(8,128)(2,1)S(1)}, bf16[4,48,1536]{2,1,0:T(8,128)(2,1)S(1)}, u32[]{:S(2)}, u32[]{:S(2)}) collective-permute-start(bf16[4,48,1536]{2,1,0:T(8,128)(2,1)S(1)} %get-tuple-element.138), channel_id=1, source_target_pairs={{0,2},{1,3},{2,0},{3,1},{4,6},{5,7},{6,4},{7,5},{8,10},{9,11},{10,... | collective-permute-start | bytes 1769480 | tf_op jit(solution)/shard_map/ppermute | solution.py:170
  410.8 60.3 %collective-permute-start.29 = (bf16[4,192,768]{2,1,0:T(8,128)(2,1)S(1)}, bf16[4,192,768]{2,1,0:T(8,128)(2,1)S(1)}, u32[]{:S(2)}, u32[]{:S(2)}) collective-permute-start(bf16[4,192,768]{2,1,0:T(8,128)(2,1)S(1)} %get-tuple-element.120), channel_id=1, source_target_pairs={{0,2},{1,3},{2,0},{3,1},{4,6},{5,7},{6,4},{7,5},{8,10},{9,11},{10,... | collective-permute-start | bytes 3538952 | tf_op jit(solution)/shard_map/ppermute | solution.py:170
  411.4 15.4 %copy-start.18 = (bf16[8,48,2304]{2,1,0:T(8,128)(2,1)S(1)}, bf16[8,48,2304]{2,1,0:T(8,128)(2,1)}, u32[]{:S(2)}) copy-start(bf16[8,48,2304]{2,1,0:T(8,128)(2,1)} %copy-done.17) | copy-start | bytes 5308420
  423.3 6.8 %collective-permute-start.11 = (bf16[48,1536]{1,0:T(8,128)(2,1)S(1)}, bf16[48,1536]{1,0:T(8,128)(2,1)S(1)}, u32[]{:S(2)}, u32[]{:S(2)}) collective-permute-start(bf16[48,1536]{1,0:T(8,128)(2,1)S(1)} %get-tuple-element.144), channel_id=1, source_target_pairs={{0,4},{1,5},{2,6},{3,7},{4,0},{5,1},{6,2},{7,3},{8,12},{9,13},{10,... | collective-permute-start | bytes 442376 | tf_op jit(solution)/shard_map/ppermute | solution.py:175
  423.3 11.8 %collective-permute-start.12 = (bf16[48,1536]{1,0:T(8,128)(2,1)S(1)}, bf16[48,1536]{1,0:T(8,128)(2,1)S(1)}, u32[]{:S(2)}, u32[]{:S(2)}) collective-permute-start(bf16[48,1536]{1,0:T(8,128)(2,1)S(1)} %get-tuple-element.146), channel_id=1, source_target_pairs={{0,8},{1,9},{2,10},{3,11},{4,12},{5,13},{6,14},{7,15},{8,0},{9,1},... | collective-permute-start | bytes 442376 | tf_op jit(solution)/shard_map/ppermute | solution.py:175
  425.8 12.5 %collective-permute-start.13 = (bf16[48,1536]{1,0:T(8,128)(2,1)S(1)}, bf16[48,1536]{1,0:T(8,128)(2,1)S(1)}, u32[]{:S(2)}, u32[]{:S(2)}) collective-permute-start(bf16[48,1536]{1,0:T(8,128)(2,1)S(1)} %get-tuple-element.145), channel_id=1, source_target_pairs={{0,12},{1,13},{2,14},{3,15},{4,8},{5,9},{6,10},{7,11},{8,4},{9,5},... | collective-permute-start | bytes 442376 | tf_op jit(solution)/shard_map/ppermute | solution.py:175
  427.2 40.2 %collective-permute-start.5 = (bf16[4,48,2304]{2,1,0:T(8,128)(2,1)S(1)}, bf16[4,48,2304]{2,1,0:T(8,128)(2,1)S(1)}, u32[]{:S(2)}, u32[]{:S(2)}) collective-permute-start(bf16[4,48,2304]{2,1,0:T(8,128)(2,1)S(1)} %get-tuple-element.124), channel_id=1, source_target_pairs={{0,2},{1,3},{2,0},{3,1},{4,6},{5,7},{6,4},{7,5},{8,10},{9,11},{10,... | collective-permute-start | bytes 2654216 | tf_op jit(solution)/shard_map/ppermute | solution.py:170
  430.0 61.9 %collective-permute-start.24 = (bf16[4,48,3072]{2,1,0:T(8,128)(2,1)S(1)}, bf16[4,48,3072]{2,1,0:T(8,128)(2,1)S(1)}, u32[]{:S(2)}, u32[]{:S(2)}) collective-permute-start(bf16[4,48,3072]{2,1,0:T(8,128)(2,1)S(1)} %get-tuple-element.122), channel_id=1, source_target_pairs={{0,2},{1,3},{2,0},{3,1},{4,6},{5,7},{6,4},{7,5},{8,10},{9,11},{10,... | collective-permute-start | bytes 3538952 | tf_op jit(solution)/shard_map/ppermute | solution.py:170
  435.1 7.8 %collective-permute-start.37 = (bf16[256,768]{1,0:T(8,128)(2,1)S(1)}, bf16[256,768]{1,0:T(8,128)(2,1)S(1)}, u32[]{:S(2)}, u32[]{:S(2)}) collective-permute-start(bf16[256,768]{1,0:T(8,128)(2,1)S(1)} %fusion.76), channel_id=1, source_target_pairs={{0,16},{16,0},{1,17},{17,1},{2,18},{18,2},{3,19},{19,3},{4,20},{20... | collective-permute-start | bytes 1179656 | tf_op jit(solution)/shard_map/ppermute | solution.py:61
  467.5 24.9 %collective-permute-start.6 = (bf16[48,2304]{1,0:T(8,128)(2,1)S(1)}, bf16[48,2304]{1,0:T(8,128)(2,1)S(1)}, u32[]{:S(2)}, u32[]{:S(2)}) collective-permute-start(bf16[48,2304]{1,0:T(8,128)(2,1)S(1)} %get-tuple-element.139), channel_id=1, source_target_pairs={{0,4},{1,5},{2,6},{3,7},{4,0},{5,1},{6,2},{7,3},{8,12},{9,13},{10,... | collective-permute-start | bytes 663560 | tf_op jit(solution)/shard_map/ppermute | solution.py:175
  467.6 25.9 %collective-permute-start.7 = (bf16[48,2304]{1,0:T(8,128)(2,1)S(1)}, bf16[48,2304]{1,0:T(8,128)(2,1)S(1)}, u32[]{:S(2)}, u32[]{:S(2)}) collective-permute-start(bf16[48,2304]{1,0:T(8,128)(2,1)S(1)} %get-tuple-element.141), channel_id=1, source_target_pairs={{0,8},{1,9},{2,10},{3,11},{4,12},{5,13},{6,14},{7,15},{8,0},{9,1},... | collective-permute-start | bytes 663560 | tf_op jit(solution)/shard_map/ppermute | solution.py:175
  470.1 26.5 %collective-permute-start.8 = (bf16[48,2304]{1,0:T(8,128)(2,1)S(1)}, bf16[48,2304]{1,0:T(8,128)(2,1)S(1)}, u32[]{:S(2)}, u32[]{:S(2)}) collective-permute-start(bf16[48,2304]{1,0:T(8,128)(2,1)S(1)} %get-tuple-element.140), channel_id=1, source_target_pairs={{0,12},{1,13},{2,14},{3,15},{4,8},{5,9},{6,10},{7,11},{8,4},{9,5},... | collective-permute-start | bytes 663560 | tf_op jit(solution)/shard_map/ppermute | solution.py:175
  471.3 25.8 %collective-permute-start.30 = (bf16[192,768]{1,0:T(8,128)(2,1)S(1)}, bf16[192,768]{1,0:T(8,128)(2,1)S(1)}, u32[]{:S(2)}, u32[]{:S(2)}) collective-permute-start(bf16[192,768]{1,0:T(8,128)(2,1)S(1)} %get-tuple-element.131), channel_id=1, source_target_pairs={{0,4},{1,5},{2,6},{3,7},{4,0},{5,1},{6,2},{7,3},{8,12},{9,13},{10,... | collective-permute-start | bytes 884744 | tf_op jit(solution)/shard_map/ppermute | solution.py:175
  491.9 21.3 %collective-permute-start.31 = (bf16[192,768]{1,0:T(8,128)(2,1)S(1)}, bf16[192,768]{1,0:T(8,128)(2,1)S(1)}, u32[]{:S(2)}, u32[]{:S(2)}) collective-permute-start(bf16[192,768]{1,0:T(8,128)(2,1)S(1)} %get-tuple-element.133), channel_id=1, source_target_pairs={{0,8},{1,9},{2,10},{3,11},{4,12},{5,13},{6,14},{7,15},{8,0},{9,1},... | collective-permute-start | bytes 884744 | tf_op jit(solution)/shard_map/ppermute | solution.py:175
  492.5 40.3 %collective-permute-start.32 = (bf16[192,768]{1,0:T(8,128)(2,1)S(1)}, bf16[192,768]{1,0:T(8,128)(2,1)S(1)}, u32[]{:S(2)}, u32[]{:S(2)}) collective-permute-start(bf16[192,768]{1,0:T(8,128)(2,1)S(1)} %get-tuple-element.132), channel_id=1, source_target_pairs={{0,12},{1,13},{2,14},{3,15},{4,8},{5,9},{6,10},{7,11},{8,4},{9,5},... | collective-permute-start | bytes 884744 | tf_op jit(solution)/shard_map/ppermute | solution.py:175
  493.6 40.2 %collective-permute-start.25 = (bf16[48,3072]{1,0:T(8,128)(2,1)S(1)}, bf16[48,3072]{1,0:T(8,128)(2,1)S(1)}, u32[]{:S(2)}, u32[]{:S(2)}) collective-permute-start(bf16[48,3072]{1,0:T(8,128)(2,1)S(1)} %get-tuple-element.134), channel_id=1, source_target_pairs={{0,4},{1,5},{2,6},{3,7},{4,0},{5,1},{6,2},{7,3},{8,12},{9,13},{10,... | collective-permute-start | bytes 884744 | tf_op jit(solution)/shard_map/ppermute | solution.py:175
  496.6 41.0 %collective-permute-start.26 = (bf16[48,3072]{1,0:T(8,128)(2,1)S(1)}, bf16[48,3072]{1,0:T(8,128)(2,1)S(1)}, u32[]{:S(2)}, u32[]{:S(2)}) collective-permute-start(bf16[48,3072]{1,0:T(8,128)(2,1)S(1)} %get-tuple-element.136), channel_id=1, source_target_pairs={{0,8},{1,9},{2,10},{3,11},{4,12},{5,13},{6,14},{7,15},{8,0},{9,1},... | collective-permute-start | bytes 884744 | tf_op jit(solution)/shard_map/ppermute | solution.py:175
  497.2 46.9 %collective-permute-start.27 = (bf16[48,3072]{1,0:T(8,128)(2,1)S(1)}, bf16[48,3072]{1,0:T(8,128)(2,1)S(1)}, u32[]{:S(2)}, u32[]{:S(2)}) collective-permute-start(bf16[48,3072]{1,0:T(8,128)(2,1)S(1)} %get-tuple-element.135), channel_id=1, source_target_pairs={{0,12},{1,13},{2,14},{3,15},{4,8},{5,9},{6,10},{7,11},{8,4},{9,5},... | collective-permute-start | bytes 884744 | tf_op jit(solution)/shard_map/ppermute | solution.py:175
  (43 other events, 151.8 us)
Sparse Core Ops, SparseCore 0:
  10.8 67.2 all-gather.3
  80.4 51.8 all-gather.5
  134.6 51.6 all-gather.7

commit v2 on v1

--- a/solution.py
+++ b/solution.py
@@ -159,30 +159,76 @@
     )(lhs, rhs)
 
 
-def scatter_sum(keep, send, count):
-    received = lax.ppermute(send, "pages", flip(count, 1))
-    quarter = keep.shape[0] // 2
-
-    def added(part):
-        return (keep[part].astype(single) + received[part].astype(single)).astype(half)
-
-    send = added(slice(quarter, None))
-    received_x = lax.ppermute(send, "pages", flip(count, 2))
-    keep = added(slice(0, quarter))
-    total = keep[0].astype(single) + received_x[0].astype(single)
-    for slot in range(1, quarter):
-        part = (keep[slot].astype(single) + received_x[slot].astype(single)).astype(half)
-        total = total + lax.ppermute(part, "pages", flip(count, 4 * slot)).astype(single)
-    return total
-
-
-def summed_rows(lhs, rhs, count, tile, by_rows=False):
-    if count == 16:
-        return scatter_sum(*weight_grads(lhs, rhs, count, tile, by_rows), count)[None]
-    if rhs.ndim == 3:
-        rhs = jnp.concatenate(list(rhs), -1)
-    local = times_over_rows(lhs, rhs).astype(half)
-    return lax.psum_scatter(local[None], "pages", scatter_dimension=1, tiled=True).astype(single)
+class RowSum:
+    def __init__(self, lhs, rhs, count, tile, by_rows=False):
+        self.count = count
+        self.split = count == 16
+        if self.split:
+            self.keep, self.send = weight_grads(lhs, rhs, count, tile, by_rows)
+            self.held = [self.send]
+        else:
+            if rhs.ndim == 3:
+                rhs = jnp.concatenate(list(rhs), -1)
+            local = times_over_rows(lhs, rhs).astype(half)
+            local = lax.psum_scatter(local[None], "pages", scatter_dimension=1, tiled=True)
+            self.held = [local.astype(single)]
+
+    def cores(self):
+        if self.split:
+            self.held = [lax.ppermute(self.held[0], "pages", flip(self.count, 1))]
+
+    def across_x(self):
+        if self.split:
+            quarter = self.keep.shape[0] // 2
+            received = self.held[0]
+            added = [
+                (self.keep[part].astype(single) + received[part].astype(single)).astype(half)
+                for part in (slice(0, quarter), slice(quarter, None))
+            ]
+            self.keep = added[0]
+            self.held = [lax.ppermute(added[1], "pages", flip(self.count, 2))]
+
+    def across_z(self):
+        if self.split:
+            received = self.held[0]
+            self.total = self.keep[0].astype(single) + received[0].astype(single)
+            self.held = []
+            for slot in range(1, self.keep.shape[0]):
+                part = self.keep[slot].astype(single) + received[slot].astype(single)
+                self.held.append(
+                    lax.ppermute(part.astype(half), "pages", flip(self.count, 4 * slot))
+                )
+
+    def result(self):
+        if not self.split:
+            return self.held[0]
+        total = self.total
+        for part in self.held:
+            total = total + part.astype(single)
+        return total[None]
+
+
+def after(array, *sums):
+    held = [part for one in sums for part in one.held]
+    array, *held = lax.optimization_barrier((array, *held))
+    for one in sums:
+        one.held, held = held[: len(one.held)], held[len(one.held) :]
+    return array
+
+
+def sum_table(array, count):
+    rows = array.shape[0] // 2
+    core = lax.rem(lax.axis_index("pages"), 2)
+    mine = lax.dynamic_slice_in_dim(array, core * rows, rows, 0)
+    other = lax.dynamic_slice_in_dim(array, (1 - core) * rows, rows, 0)
+    mine = mine + lax.ppermute(other.astype(half), "pages", flip(count, 1)).astype(single)
+    for bit in bits_of(count)[1:]:
+        mine = rounded(mine, half)
+        mine = mine + lax.ppermute(mine.astype(half), "pages", flip(count, bit)).astype(single)
+    mine = rounded(mine, half)
+    mine = rounded(mine + swap_streams(mine.astype(half)).astype(single), half)
+    other = lax.ppermute(mine.astype(half), "pages", flip(count, 1)).astype(single)
+    return jnp.where(core == 0, jnp.concatenate([mine, other]), jnp.concatenate([other, mine]))
 
 
 def wide_rows(first, second, extra, which, size):
@@ -526,30 +572,56 @@
     upstream = output_cotangent[0].astype(single)
     grad_resid_two = norm_back(upstream * gain_two, normed_two, inverse_two)
     grad_branch = grad_resid_two.astype(half)
-    grad_down = summed_rows(active_half, grad_branch, count, width, by_rows=True)
+    down_sum = RowSum(active_half, grad_branch, count, width, by_rows=True)
+    grad_branch = after(grad_branch, down_sum)
+    down_sum.cores()
     grad_pre = (times_transposed(grad_branch, full_down) * slope).astype(half)
+    grad_pre = after(grad_pre, down_sum)
+    down_sum.across_x()
     grad_hidden = grad_resid_two + times_transposed(grad_pre, full_up)
     grad_resid_one = norm_back(grad_hidden * gain_one, normed_one, inverse_one)
-    grad_up = summed_rows(hidden_half, grad_pre, count, width)
+    sent, hidden_back = lax.optimization_barrier((grad_resid_one.astype(half), hidden_half))
+    up_sum = RowSum(hidden_back, grad_pre, count, width)
 
     grad_attention, before = [], None
     for page in range(page_count):
-        part = grad_resid_one[page * SLOTS : (page + 1) * SLOTS]
-        part = (part + swap_streams(part.astype(half)).astype(single)).astype(half)
-        grad_attention.append(part)
+        rows = slice(page * SLOTS, (page + 1) * SLOTS)
+        part = grad_resid_one[rows] + swap_streams(sent[rows]).astype(single)
+        grad_attention.append(part.astype(half))
+    up_sum.cores()
+    grad_attention[0] = after(grad_attention[0], down_sum, up_sum)
+    down_sum.across_z()
+    up_sum.across_x()
+    output_sum = None
+    for page in range(page_count):
+        part = grad_attention[page]
+        if page == page_count - 1:
+            output_sum = RowSum(mixture, jnp.concatenate(grad_attention, 0), count, width)
+            part = after(part, down_sum, output_sum)
+            output_sum.cores()
         before = attend_page_back(
             page, joint_half, spatial_rows, cells, cells_t, keyx, rel, logs[page], part, full_output,
             heads, before,
         )
     grad_rows, cell_q, cell_k, bin_sums = before
     grad_attention = jnp.concatenate(grad_attention, 0)
-    grad_output = summed_rows(mixture, grad_attention, count, width)
-    grad_joint = summed_rows(inputs, grad_rows, count, width)
+    grad_rows = after(grad_rows, up_sum, output_sum)
+    up_sum.across_z()
+    joint_sum = RowSum(inputs, grad_rows, count, width)
     cell_half = jnp.concatenate([cell_q, cell_k], 1).astype(half)
-    grad_spatial = summed_rows(spatial_table, cell_half, count, width)
-    grad_table = sum_pages(times_transposed(cell_half, full_spatial), count, half)
-    grad_table = rounded(grad_table, half)
-    grad_table = grad_table + swap_streams(grad_table.astype(half)).astype(single)
+    cell_half = after(cell_half, joint_sum)
+    joint_sum.cores()
+    spatial_sum = RowSum(spatial_table, cell_half, count, width)
+    cell_half = after(cell_half, joint_sum, spatial_sum)
+    joint_sum.across_x()
+    spatial_sum.cores()
+    output_sum.across_x()
+    spatial_sum.across_x()
+    joint_sum.across_z()
+    output_sum.across_z()
+    spatial_sum.across_z()
+    grad_table = sum_table(times_transposed(cell_half, full_spatial), count)
+    grad_rows = lax.optimization_barrier((grad_rows, cell_half))[0]
     grad_features = input_grad(grad_rows, full_joint, grad_resid_one)
 
     small = [
@@ -573,16 +645,16 @@
     return (
         layer_output[None],
         grad_features[None],
-        grad_joint,
-        grad_spatial,
+        joint_sum.result(),
+        spatial_sum.result(),
         small[7].reshape(relative_table.shape),
-        grad_output,
+        output_sum.result(),
         small[2][None],
         small[0][None],
         small[1][None],
-        grad_up,
+        up_sum.result(),
         small[3][None],
-        grad_down,
+        down_sum.result(),
         small[4][None],
         small[5][None],
         small[6][None],

time: 562 us -> 505 us (0.90)
  waiting for transfers between devices: 217 us -> 193 us
  local copies, waits for them, and re-layouts: 53.9 us -> 35.9 us
  other arithmetic: 58.2 us -> 45.2 us
    ppermute x25 -> x30, waiting for transfers between devices: 110 us -> 53.5 us  [the longest x15 36.2 us: across_z(): lax.ppermute(part.astype(half), 'pages', flip(self.count, 4 * slot))]
    ppermute x5, waiting for transfers between devices: 19.1 us -> 50.2 us  [swap_streams(): return lax.ppermute(array, 'stream', [(0, 1), (1, 0)])]
    mul x1 -> x0, other arithmetic: 13.1 us -> none  [norm_back(): inverse * (grad_normed - jnp.mean(grad_normed, -1, keepdims=True) - norme...]
    unnamed x149 -> x133, local copies, waits for them, and re-layouts: 36.8 us -> 24.1 us
    ppermute x8 -> x4, starting transfers between devices: 11.1 us -> 3.08 us  [sum_pages(): received = lax.ppermute(array.astype(kept), 'pages', flip(count, bit))]
    ppermute x25 -> x30, starting transfers between devices: 24.3 us -> 27.1 us  [the longest x15 18.1 us: across_z(): lax.ppermute(part.astype(half), 'pages', flip(self.count, 4 * slot))]
    convert_element_type x15 -> x19, other arithmetic: 15.6 us -> 17.9 us  [the longest x5 8.34 us: across_x(): (self.keep[part].astype(single) + received[part].astype(single)).astype(h...]
  transfers between devices with their start and end apart: 41 -> 42, of which waited for: 20 -> 19; matrix products, arithmetic and copies ran while one was open for 19% -> 17% of each run, Pallas kernels for 18% -> 17%
where the time goes in v2:
time: 505 us; the launch traced here: 496 us
  waiting for transfers between devices  193 us (38%)
  Pallas kernels  101 us (20%)
  matrix products  68.3 us (14%)
  other arithmetic  45.2 us (9%)
  starting transfers between devices  36.7 us (7%)
  local copies, waits for them, and re-layouts  35.9 us (7%)
  between operations  15.4 us (3%)
    all_gather x1, waiting for transfers between devices, body(): early = lax.all_gather(early, 'pages', axis=1, tiled=True)[0]  58.3 us
    ppermute x5, waiting for transfers between devices, swap_streams(): return lax.ppermute(array, 'stream', [(0, 1), (1, 0)])  50.2 us
    ppermute x15, waiting for transfers between devices, across_z(): lax.ppermute(part.astype(half), 'pages', flip(self.count, 4 * slot))  36.2 us
    pallas_call x2, Pallas kernels, attend_page_back(): pl.pallas_call(functools.partial(backward_kernel, scale=size ** (-0.5), s...  35.9 us
    dot_general x3, matrix products, times_transposed(): lax.dot_general(left, right, (((1,), (1,)), ((), ())), preferred_element_...  35.7 us
    dot_general x4, matrix products, times(): return jnp.dot(left, right, preferred_element_type=single)  31.5 us
    pallas_call x5, Pallas kernels, weight_grads(): pl.pallas_call(functools.partial(grads_kernel, blocks=blocks, by_rows=by_...  30.3 us
    pallas_call x2, Pallas kernels, attend_page(): pl.pallas_call(functools.partial(forward_kernel, scale=size ** (-0.5), si...  27.3 us
  transfers between devices with their start and end apart: 42, of which 19 were waited for; matrix products, arithmetic and copies ran while one was open for 17% of the time, Pallas kernels for 17%

profile of v2, /device:TPU:8, one launch (start us, length us, event | category | flops | bytes accessed | tf_op | source)
XLA Modules:
  0.0 495.9 jit_solution(1392593042590271402)
XLA Ops:
  7.2 1.8 pad_maximum_fusion.3
  12.8 1.8 copy.49
  16.0 3.6 concatenate.51.keyx_ref
  19.8 58.3 %all-gather.4.cloned.1.call-done = bf16[1,768,4608]{2,1,0:T(8,128)(2,1)} async-done(((bf16[1,48,4608]{2,1,0:T(8,128)(2,1)}), bf16[1,768,4608]{2,1,0:T(8,128)(2,1)}) %all-gather.4.cloned.1.call-update) | async-done | bytes 7077904 | tf_op jit(solution)/shard_map/all_gather | solution.py:538
  79.6 2.4 fusion.29.sq_ref.sk_ref
  82.1 6.0 %fusion.6.q_ref.k_ref.v_ref = bf16[1024,2304]{1,0:T(8,128)(2,1)S(1)} fusion(bf16[1,1024,768]{2,1,0:T(8,128)(2,1)S(1)} %copy-done.12, bf16[768,4608]{1,0:T(8,128)(2,1)} %bitcast.247), kind=kOutput, calls=%fused_computation.11 | convolution fusion | flops 3626237952 | bytes 9830400 | tf_op jit(solution)/shard_map/dot_general | solution.py:25
  88.1 13.7 %attend_page.2 = (bf16[512,768]{1,0:T(8,128)(2,1)S(1)}, f32[512,768]{1,0:T(8,128)S(1)}, bf16[512,768]{1,0:T(8,128)(2,1)}, f32[12,512]{1,0:T(8,128)S(1)}) custom-call(bf16[1024,2304]{1,0:T(8,128)(2,1)S(1)} %fusion.6.q_ref.k_ref.v_ref, bf16[1024,2304]{1,0:T(8,128)(2,1)S(1)} %fusion.6.q_ref.k_ref.v_ref, bf16[1024,2304]{1,0:T(8,128)(2,1)S(1)} %fusion.6.q_ref.k_ref.v_ref, ...), custom_call_target="tpu_custom_call" | custom-call | flops 2415919104 | bytes 4718592 | tf_op jit(solution)/shard_map/attend_page/pallas_call | solution.py:283
  103.9 1.5 collective-permute-start
  105.4 13.6 %attend_page.3 = (bf16[512,768]{1,0:T(8,128)(2,1)S(1)}, f32[512,768]{1,0:T(8,128)S(1)}, bf16[512,768]{1,0:T(8,128)(2,1)}, f32[12,512]{1,0:T(8,128)S(1)}) custom-call(bf16[1024,2304]{1,0:T(8,128)(2,1)S(1)} %fusion.6.q_ref.k_ref.v_ref, bf16[1024,2304]{1,0:T(8,128)(2,1)S(1)} %fusion.6.q_ref.k_ref.v_ref, bf16[1024,2304]{1,0:T(8,128)(2,1)S(1)} %fusion.6.q_ref.k_ref.v_ref, ...), custom_call_target="tpu_custom_call" | custom-call | flops 2415919104 | bytes 4718592 | tf_op jit(solution)/shard_map/attend_page/pallas_call | solution.py:283
  121.8 2.2 collective-permute-done
  124.0 1.9 convert_add_fusion.1
  125.9 14.9 %collective-permute-done.1 = bf16[512,768]{1,0:T(8,128)(2,1)} collective-permute-done((bf16[512,768]{1,0:T(8,128)(2,1)}, bf16[512,768]{1,0:T(8,128)(2,1)}, u32[]{:S(2)}, u32[]{:S(2)}) %collective-permute-start.1) | collective-permute-done | bytes 786464 | tf_op jit(solution)/shard_map/ppermute | solution.py:61
  143.4 1.7 copy-done.29
  145.6 13.8 %multiply_convert_fusion = (bf16[1024,3072]{1,0:T(8,128)(2,1)}, f32[1024,3072]{1,0:T(8,128)}) fusion(f32[3072]{0:T(1024)S(1)} %bitcast.263, bf16[1,768,3072]{2,1,0:T(8,128)(2,1)} %all-gather.6.cloned.1.call-done, f32[1,512,768]{2,1,0:T(8,128)} %bitcast.243, f32[1,512,768]{2,1,0:T(8,128)} %bitcast.242, bf16[1,1024,768]{2,1,0:T(8,128)(2,1)} %param.24, ...), kind=kOutput, calls=%fused_computation.8 | convolution fusion | flops 4857004032 | bytes 28338176 | tf_op jit(solution)/shard_map/dot_general | solution.py:25
  159.4 26.9 %all-gather.8.cloned.1.call-done = bf16[1,3072,768]{2,1,0:T(8,128)(2,1)} async-done(((bf16[1,192,768]{2,1,0:T(8,128)(2,1)}), bf16[1,3072,768]{2,1,0:T(8,128)(2,1)}) %all-gather.8.cloned.1.call-update) | async-done | bytes 4718608 | tf_op jit(solution)/shard_map/all_gather | solution.py:543
  186.3 9.3 %fusion.106 = (f32[1024]{0:T(1024)S(1)}, f32[1024,768]{1,0:T(8,128)S(1)}) fusion(f32[768]{0:T(1024)S(1)} %reduce.10, bf16[1024,3072]{1,0:T(8,128)(2,1)} %get-tuple-element.211.lhs_ref, bf16[1,3072,768]{2,1,0:T(8,128)(2,1)} %all-gather.8.cloned.1.call-done, f32[768]{0:T(1024)S(1)} %reduce.9, f32[768]{0:T(1024)S(1)} %reduce.8, ...), kind=kOutput, calls=%fused_computation.219 | convolution fusion | flops 4837342208 | bytes 17323008 | tf_op jit(solution)/shard_map/dot_general | solution.py:25
  196.2 2.0 copy-done.32
  199.7 2.3 fusion.98
  201.9 8.4 %weight_grads.5 = (bf16[8,192,768]{2,1,0:T(8,128)(2,1)S(1)}, bf16[8,192,768]{2,1,0:T(8,128)(2,1)S(1)}) custom-call(bf16[1024,3072]{1,0:T(8,128)(2,1)S(1)} %bitcast.241, bf16[1024,768]{1,0:T(8,128)(2,1)S(1)} %get-tuple-element.107.rhs_ref), custom_call_target="tpu_custom_call" | custom-call | flops 4831838208 | bytes 12582912 | tf_op jit(solution)/shard_map/weight_grads/pallas_call | solution.py:142
  210.7 11.5 %fusion.5.rhs_ref = bf16[1024,3072]{1,0:T(8,128)(2,1)S(1)} fusion(f32[1024,3072]{1,0:T(8,128)} %get-tuple-element.212, bf16[1024,768]{1,0:T(8,128)(2,1)S(1)} %get-tuple-element.107.rhs_ref, f32[3072]{0:T(1024)S(1)} %bitcast.264, bf16[1,3072,768]{2,1,0:T(8,128)(2,1)} %all-gather.8.cloned.1.call-done), kind=kOutput, calls=%fused_computation.6 | convolution fusion | flops 4866441216 | bytes 25178112 | tf_op jit(solution)/shard_map/dot_general | solution.py:33
  222.2 21.8 %multiply_reduce_fusion = (f32[768]{0:T(1024)S(1)}, f32[1024]{0:T(1024)S(1)}, f32[1024]{0:T(1024)S(1)}, f32[768]{0:T(1024)S(1)}, bf16[1024,768]{1,0:T(8,128)(2,1)}, /*index=5*/f32[1024,768]{1,0:T(8,128)}) fusion(f32[1024,768]{1,0:T(8,128)S(1)} %copy-done.30, f32[1024]{0:T(1024)S(1)} %add_rsqrt_fusion.1, f32[1024]{0:T(1024)S(1)} %broadcast_multiply_fusion.5, ...), kind=kOutput, calls=%fused_computation.39 | convolution fusion | flops 4848349184 | bytes 23641088 | tf_op jit(solution)/shard_map/dot_general | solution.py:33
  244.0 4.4 fusion.101
  250.3 9.2 %weight_grads.6 = (bf16[8,48,3072]{2,1,0:T(8,128)(2,1)S(1)}, bf16[8,48,3072]{2,1,0:T(8,128)(2,1)}) custom-call(bf16[1024,768]{1,0:T(8,128)(2,1)S(1)} %copy-done.28, bf16[1024,3072]{1,0:T(8,128)(2,1)S(1)} %copy-done.6), custom_call_target="tpu_custom_call" | custom-call | flops 4831838208 | bytes 12582912 | tf_op jit(solution)/shard_map/weight_grads/pallas_call | solution.py:142
  259.8 1.7 convert_reduce_fusion.1
  261.6 2.4 pad_maximum_fusion.lhs_ref
  264.0 2.3 add_convert_fusion.3
  267.1 1.5 collective-permute-start.3
  270.4 17.2 %collective-permute-done.3 = bf16[512,768]{1,0:T(8,128)(2,1)S(1)} collective-permute-done((bf16[512,768]{1,0:T(8,128)(2,1)S(1)}, bf16[512,768]{1,0:T(8,128)(2,1)S(1)}, u32[]{:S(2)}, u32[]{:S(2)}) %collective-permute-start.3) | collective-permute-done | bytes 786464 | tf_op jit(solution)/shard_map/ppermute | solution.py:61
  287.6 15.9 %collective-permute-done.4 = bf16[512,768]{1,0:T(8,128)(2,1)S(1)} collective-permute-done((bf16[512,768]{1,0:T(8,128)(2,1)S(1)}, bf16[512,768]{1,0:T(8,128)(2,1)S(1)}, u32[]{:S(2)}, u32[]{:S(2)}) %collective-permute-start.4) | collective-permute-done | bytes 786464 | tf_op jit(solution)/shard_map/ppermute | solution.py:61
  303.8 2.3 add_convert_fusion.1
  308.4 1.8 collective-permute-start.8
  311.7 17.9 %attend_page_back.2 = (bf16[3,1024,768]{2,1,0:T(8,128)(2,1)S(1)}, f32[256,768]{1,0:T(8,128)S(1)}, f32[256,768]{1,0:T(8,128)S(1)}, f32[6,96,128]{2,1,0:T(8,128)S(1)}) custom-call(bf16[1024,2304]{1,0:T(8,128)(2,1)S(1)} %bitcast.235, bf16[1024,2304]{1,0:T(8,128)(2,1)S(1)} %bitcast.235, bf16[1024,2304]{1,0:T(8,128)(2,1)S(1)} %bitcast.235, ...), custom_call_target="tpu_custom_call" | custom-call | flops 6442450944 | bytes 7864320 | tf_op jit(solution)/shard_map/attend_page_back/pallas_call | solution.py:387
  331.0 3.4 weight_grads.7
  335.8 18.0 %attend_page_back.3 = (bf16[3,1024,768]{2,1,0:T(8,128)(2,1)S(1)}, f32[256,768]{1,0:T(8,128)S(1)}, f32[256,768]{1,0:T(8,128)S(1)}, f32[6,96,128]{2,1,0:T(8,128)S(1)}) custom-call(bf16[1024,2304]{1,0:T(8,128)(2,1)S(1)} %bitcast.235, bf16[1024,2304]{1,0:T(8,128)(2,1)S(1)} %bitcast.235, ...), custom_call_target="tpu_custom_call", output_to_operand_aliasing={{0}: (12, {}), {1}: (13, {}), {2}: (14, {}), {3}: (15, {})} | custom-call | flops 6442450944 | bytes 7864320 | tf_op jit(solution)/shard_map/attend_page_back/pallas_call | solution.py:387
  353.9 2.2 copy-done.3
  362.9 2.4 collective-permute-done.23
  367.0 2.3 copy-done.4
  369.3 6.7 %weight_grads.8 = (bf16[8,48,2304]{2,1,0:T(8,128)(2,1)S(1)}, bf16[8,48,2304]{2,1,0:T(8,128)(2,1)}) custom-call(bf16[1024,768]{1,0:T(8,128)(2,1)S(1)} %bitcast.238, bf16[3,1024,768]{2,1,0:T(8,128)(2,1)S(1)} %copy-done.4), custom_call_target="tpu_custom_call" | custom-call | flops 3623878656 | bytes 9830400 | tf_op jit(solution)/shard_map/weight_grads/pallas_call | solution.py:142
  377.4 2.3 slice.447.weight_ref
  380.5 2.2 collective-permute-start.25
  382.7 2.1 fusion.51
  392.3 1.6 fusion.64
  393.9 2.2 collective-permute-start.30
  397.7 2.5 weight_grads.9
  400.3 2.9 collective-permute-start.27
  403.6 2.5 fusion.30
  406.1 2.6 collective-permute-done.30
  409.7 7.7 %collective-permute-done.31 = bf16[48,3072]{1,0:T(8,128)(2,1)S(1)} collective-permute-done((bf16[48,3072]{1,0:T(8,128)(2,1)S(1)}, bf16[48,3072]{1,0:T(8,128)(2,1)S(1)}, u32[]{:S(2)}, u32[]{:S(2)}) %collective-permute-start.31) | collective-permute-done | bytes 294944 | tf_op jit(solution)/shard_map/ppermute | solution.py:199
  417.4 10.3 %collective-permute-done.32 = bf16[48,3072]{1,0:T(8,128)(2,1)S(1)} collective-permute-done((bf16[48,3072]{1,0:T(8,128)(2,1)S(1)}, bf16[48,3072]{1,0:T(8,128)(2,1)S(1)}, u32[]{:S(2)}, u32[]{:S(2)}) %collective-permute-start.32) | collective-permute-done | bytes 294944 | tf_op jit(solution)/shard_map/ppermute | solution.py:199
  427.7 2.0 fusion.54
  429.8 1.5 collective-permute-start.34
  432.0 3.5 collective-permute-done.34
  435.7 2.0 add_convert_fusion.6
  437.7 1.5 collective-permute-start.13
  439.2 3.1 collective-permute-done.35
  442.5 7.4 %input_grad.1 = f32[1024,768]{1,0:T(8,128)} custom-call(bf16[3,1024,768]{2,1,0:T(8,128)(2,1)S(1)} %bitcast.237, bf16[768,2304]{1,0:T(8,128)(2,1)S(1)} %slice.447.weight_ref, f32[1024,768]{1,0:T(8,128)S(1)} %copy-done.2), custom_call_target="tpu_custom_call" | custom-call | flops 3623878656 | bytes 11010048 | tf_op jit(solution)/shard_map/input_grad/pallas_call | solution.py:442
  449.9 2.1 collective-permute-start.37
  452.4 2.0 collective-permute-start.18
  454.4 5.9 %collective-permute-done.13 = bf16[4,48,2304]{2,1,0:T(8,128)(2,1)S(1)} collective-permute-done((bf16[4,48,2304]{2,1,0:T(8,128)(2,1)S(1)}, bf16[4,48,2304]{2,1,0:T(8,128)(2,1)S(1)}, u32[]{:S(2)}, u32[]{:S(2)}) %collective-permute-start.13) | collective-permute-done | bytes 884768 | tf_op jit(solution)/shard_map/ppermute | solution.py:189
  460.4 2.1 collective-permute-start.14
  464.2 4.7 collective-permute-done.18
  469.0 1.8 collective-permute-start.19
  471.6 2.9 collective-permute-done.15
  474.9 10.1 %collective-permute-done.16 = bf16[48,2304]{1,0:T(8,128)(2,1)S(1)} collective-permute-done((bf16[48,2304]{1,0:T(8,128)(2,1)S(1)}, bf16[48,2304]{1,0:T(8,128)(2,1)S(1)}, u32[]{:S(2)}, u32[]{:S(2)}) %collective-permute-start.16) | collective-permute-done | bytes 221216 | tf_op jit(solution)/shard_map/ppermute | solution.py:199
  (276 shorter events, 57.9 us)
Async XLA Ops:
  7.2 70.9 %all-gather.4.cloned.1.call-start = ((), (), s32[]{:S(2)}) async-start(), calls=%async_computation | async-start | bytes 7520256 | tf_op jit(solution)/shard_map/all_gather | solution.py:538
  9.1 136.5 %all-gather.6.cloned.1.call-start = ((), (), s32[]{:S(2)}) async-start(), calls=%async_computation.1 | async-start | bytes 5013504 | tf_op jit(solution)/shard_map/all_gather | solution.py:542
  9.8 176.5 %all-gather.8.cloned.1.call-start = ((), (), s32[]{:S(2)}) async-start(), calls=%async_computation.2 | async-start | bytes 5013504 | tf_op jit(solution)/shard_map/all_gather | solution.py:543
  15.4 64.2 %copy-start.26 = (bf16[256,768]{1,0:T(8,128)(2,1)S(1)}, bf16[256,768]{1,0:T(8,128)(2,1)}, u32[]{:S(2)}) copy-start(bf16[256,768]{1,0:T(8,128)(2,1)} %lhs_ref.1) | copy-start | bytes 1179652
  88.1 17.3 %copy-start = (bf16[1024,2304]{1,0:T(8,128)(2,1)}, bf16[1024,2304]{1,0:T(8,128)(2,1)S(1)}, u32[]{:S(2)}) copy-start(bf16[1024,2304]{1,0:T(8,128)(2,1)S(1)} %fusion.6.q_ref.k_ref.v_ref) | copy-start | bytes 14155780
  103.9 17.8 %copy-start.46 = (f32[1,768]{1,0:T(1,128)S(1)}, f32[1,768]{1,0:T(1,128)}, u32[]{:S(2)}) copy-start(f32[1,768]{1,0:T(1,128)} %param.33) | copy-start | bytes 9220
  103.9 17.8 %copy-start.47 = (f32[1,768]{1,0:T(1,128)S(1)}, f32[1,768]{1,0:T(1,128)}, u32[]{:S(2)}) copy-start(f32[1,768]{1,0:T(1,128)} %param.34) | copy-start | bytes 9220
  103.9 17.8 %copy-start.48 = (f32[1,768]{1,0:T(1,128)S(1)}, f32[1,768]{1,0:T(1,128)}, u32[]{:S(2)}) copy-start(f32[1,768]{1,0:T(1,128)} %param.38) | copy-start | bytes 9220
  103.9 17.8 %copy-start.49 = (f32[1,768]{1,0:T(1,128)S(1)}, f32[1,768]{1,0:T(1,128)}, u32[]{:S(2)}) copy-start(f32[1,768]{1,0:T(1,128)} %param.39) | copy-start | bytes 9220
  103.9 17.9 %copy-start.50 = (f32[1,768]{1,0:T(1,128)S(1)}, f32[1,768]{1,0:T(1,128)}, u32[]{:S(2)}) copy-start(f32[1,768]{1,0:T(1,128)} %param.40) | copy-start | bytes 9220
  103.9 20.1 %collective-permute-start = (bf16[512,768]{1,0:T(8,128)(2,1)}, bf16[512,768]{1,0:T(8,128)(2,1)}, u32[]{:S(2)}, u32[]{:S(2)}) collective-permute-start(bf16[512,768]{1,0:T(8,128)(2,1)} %get-tuple-element.102), channel_id=1, source_target_pairs={{0,16},{16,0},{1,17},{17,1},{2,18},{18,2},{3,19},{19,3},{4,20},{20... | collective-permute-start | bytes 2359304 | tf_op jit(solution)/shard_map/ppermute | solution.py:61
  121.1 19.8 %collective-permute-start.1 = (bf16[512,768]{1,0:T(8,128)(2,1)}, bf16[512,768]{1,0:T(8,128)(2,1)}, u32[]{:S(2)}, u32[]{:S(2)}) collective-permute-start(bf16[512,768]{1,0:T(8,128)(2,1)} %get-tuple-element.104), channel_id=1, source_target_pairs={{0,16},{16,0},{1,17},{17,1},{2,18},{18,2},{3,19},{19,3},{4,20},{20... | collective-permute-start | bytes 2359304 | tf_op jit(solution)/shard_map/ppermute | solution.py:61
  121.8 19.1 %copy-start.18 = (f32[512,768]{1,0:T(8,128)S(1)}, f32[512,768]{1,0:T(8,128)}, u32[]{:S(2)}) copy-start(f32[512,768]{1,0:T(8,128)} %copy-done.17) | copy-start | bytes 4718596
  124.0 18.2 %copy-start.13 = (bf16[1,1024,768]{2,1,0:T(8,128)(2,1)S(1)}, bf16[1,1024,768]{2,1,0:T(8,128)(2,1)}, u32[]{:S(2)}) copy-start(bf16[1,1024,768]{2,1,0:T(8,128)(2,1)} %param.24) | copy-start | bytes 4718596
  125.9 16.7 %copy-start.34 = (f32[512,768]{1,0:T(8,128)}, f32[512,768]{1,0:T(8,128)S(1)}, u32[]{:S(2)}) copy-start(f32[512,768]{1,0:T(8,128)S(1)} %convert_add_fusion.1) | copy-start | bytes 4718596
  210.4 11.8 %collective-permute-start.2 = (bf16[8,192,768]{2,1,0:T(8,128)(2,1)S(1)}, bf16[8,192,768]{2,1,0:T(8,128)(2,1)}, u32[]{:S(2)}, u32[]{:S(2)}) collective-permute-start(bf16[8,192,768]{2,1,0:T(8,128)(2,1)S(1)} %get-tuple-element.108), channel_id=1, source_target_pairs={{0,1},{1,0},{2,3},{3,2},{4,5},{5,4},{6,7},{7,6},{8,9},{9,8},{10,11... | collective-permute-start | bytes 7077896 | tf_op jit(solution)/shard_map/ppermute | solution.py:178
  210.7 11.5 %copy-start.30 = (f32[1024,768]{1,0:T(8,128)S(1)}, f32[1024,768]{1,0:T(8,128)}, u32[]{:S(2)}) copy-start(f32[1024,768]{1,0:T(8,128)} %copy-done.29) | copy-start | bytes 9437188
  222.2 21.8 %copy-start.5 = (bf16[1024,3072]{1,0:T(8,128)(2,1)}, bf16[1024,3072]{1,0:T(8,128)(2,1)S(1)}, u32[]{:S(2)}) copy-start(bf16[1024,3072]{1,0:T(8,128)(2,1)S(1)} %fusion.5.rhs_ref) | copy-start | bytes 18874372
  248.4 55.0 %copy-start.1 = (f32[1024,768]{1,0:T(8,128)}, f32[1024,768]{1,0:T(8,128)S(1)}, u32[]{:S(2)}) copy-start(f32[1024,768]{1,0:T(8,128)S(1)} %get-tuple-element.162.resid_ref) | copy-start | bytes 9437188
  259.5 44.3 %collective-permute-start.6 = (bf16[8,48,3072]{2,1,0:T(8,128)(2,1)}, bf16[8,48,3072]{2,1,0:T(8,128)(2,1)S(1)}, u32[]{:S(2)}, u32[]{:S(2)}) collective-permute-start(bf16[8,48,3072]{2,1,0:T(8,128)(2,1)} %get-tuple-element.114), channel_id=1, source_target_pairs={{0,1},{1,0},{2,3},{3,2},{4,5},{5,4},{6,7},{7,6},{8,9},{9,8},{10,11... | collective-permute-start | bytes 7077896 | tf_op jit(solution)/shard_map/ppermute | solution.py:178
  266.3 41.3 %copy-start.36 = (bf16[4,192,768]{2,1,0:T(8,128)(2,1)}, bf16[4,192,768]{2,1,0:T(8,128)(2,1)S(1)}, u32[]{:S(2)}) copy-start(bf16[4,192,768]{2,1,0:T(8,128)(2,1)S(1)} %get-tuple-element.170) | copy-start | bytes 3538948
  266.4 37.4 %collective-permute-start.5 = (bf16[4,192,768]{2,1,0:T(8,128)(2,1)S(1)}, bf16[4,192,768]{2,1,0:T(8,128)(2,1)S(1)}, u32[]{:S(2)}, u32[]{:S(2)}) collective-permute-start(bf16[4,192,768]{2,1,0:T(8,128)(2,1)S(1)} %get-tuple-element.169), channel_id=1, source_target_pairs={{0,2},{1,3},{2,0},{3,1},{4,6},{5,7},{6,4},{7,5},{8,10},{9,11},{10,... | collective-permute-start | bytes 3538952 | tf_op jit(solution)/shard_map/ppermute | solution.py:189
  267.1 20.5 %collective-permute-start.3 = (bf16[512,768]{1,0:T(8,128)(2,1)S(1)}, bf16[512,768]{1,0:T(8,128)(2,1)S(1)}, u32[]{:S(2)}, u32[]{:S(2)}) collective-permute-start(bf16[512,768]{1,0:T(8,128)(2,1)S(1)} %get-tuple-element.190), channel_id=1, source_target_pairs={{0,16},{16,0},{1,17},{17,1},{2,18},{18,2},{3,19},{19,3},{4,20},{20... | collective-permute-start | bytes 2359304 | tf_op jit(solution)/shard_map/ppermute | solution.py:61
  268.6 34.8 %collective-permute-start.4 = (bf16[512,768]{1,0:T(8,128)(2,1)S(1)}, bf16[512,768]{1,0:T(8,128)(2,1)S(1)}, u32[]{:S(2)}, u32[]{:S(2)}) collective-permute-start(bf16[512,768]{1,0:T(8,128)(2,1)S(1)} %get-tuple-element.189), channel_id=1, source_target_pairs={{0,16},{16,0},{1,17},{17,1},{2,18},{18,2},{3,19},{19,3},{4,20},{20... | collective-permute-start | bytes 2359304 | tf_op jit(solution)/shard_map/ppermute | solution.py:61
  306.1 60.0 %collective-permute-start.10 = (bf16[4,48,3072]{2,1,0:T(8,128)(2,1)}, bf16[4,48,3072]{2,1,0:T(8,128)(2,1)}, u32[]{:S(2)}, u32[]{:S(2)}) collective-permute-start(bf16[4,48,3072]{2,1,0:T(8,128)(2,1)} %get-tuple-element.168), channel_id=1, source_target_pairs={{0,2},{1,3},{2,0},{3,1},{4,6},{5,7},{6,4},{7,5},{8,10},{9,11},{10,... | collective-permute-start | bytes 3538952 | tf_op jit(solution)/shard_map/ppermute | solution.py:189
  307.8 26.7 %collective-permute-start.7 = (bf16[192,768]{1,0:T(8,128)(2,1)S(1)}, bf16[192,768]{1,0:T(8,128)(2,1)S(1)}, u32[]{:S(2)}, u32[]{:S(2)}) collective-permute-start(bf16[192,768]{1,0:T(8,128)(2,1)S(1)} %get-tuple-element.185), channel_id=1, source_target_pairs={{0,4},{1,5},{2,6},{3,7},{4,0},{5,1},{6,2},{7,3},{8,12},{9,13},{10,... | collective-permute-start | bytes 884744 | tf_op jit(solution)/shard_map/ppermute | solution.py:199
  308.4 26.1 %collective-permute-start.8 = (bf16[192,768]{1,0:T(8,128)(2,1)S(1)}, bf16[192,768]{1,0:T(8,128)(2,1)S(1)}, u32[]{:S(2)}, u32[]{:S(2)}) collective-permute-start(bf16[192,768]{1,0:T(8,128)(2,1)S(1)} %get-tuple-element.184), channel_id=1, source_target_pairs={{0,8},{1,9},{2,10},{3,11},{4,12},{5,13},{6,14},{7,15},{8,0},{9,1},... | collective-permute-start | bytes 884744 | tf_op jit(solution)/shard_map/ppermute | solution.py:199
  310.2 25.6 %collective-permute-start.9 = (bf16[192,768]{1,0:T(8,128)(2,1)S(1)}, bf16[192,768]{1,0:T(8,128)(2,1)S(1)}, u32[]{:S(2)}, u32[]{:S(2)}) collective-permute-start(bf16[192,768]{1,0:T(8,128)(2,1)S(1)} %get-tuple-element.183), channel_id=1, source_target_pairs={{0,12},{1,13},{2,14},{3,15},{4,8},{5,9},{6,10},{7,11},{8,4},{9,5},... | collective-permute-start | bytes 884744 | tf_op jit(solution)/shard_map/ppermute | solution.py:199
  334.5 19.4 %copy-start.23 = (bf16[8,48,768]{2,1,0:T(8,128)(2,1)}, bf16[8,48,768]{2,1,0:T(8,128)(2,1)S(1)}, u32[]{:S(2)}) copy-start(bf16[8,48,768]{2,1,0:T(8,128)(2,1)S(1)} %get-tuple-element.144) | copy-start | bytes 1769476
  334.5 19.4 %copy-start.25 = (bf16[8,48,768]{2,1,0:T(8,128)(2,1)}, bf16[8,48,768]{2,1,0:T(8,128)(2,1)S(1)}, u32[]{:S(2)}) copy-start(bf16[8,48,768]{2,1,0:T(8,128)(2,1)S(1)} %get-tuple-element.129) | copy-start | bytes 1769476
  334.5 19.4 %copy-start.39 = (bf16[192,768]{1,0:T(8,128)(2,1)}, bf16[192,768]{1,0:T(8,128)(2,1)S(1)}, u32[]{:S(2)}) copy-start(bf16[192,768]{1,0:T(8,128)(2,1)S(1)} %collective-permute-done.7) | copy-start | bytes 884740
  334.5 19.4 %copy-start.41 = (bf16[192,768]{1,0:T(8,128)(2,1)}, bf16[192,768]{1,0:T(8,128)(2,1)S(1)}, u32[]{:S(2)}) copy-start(bf16[192,768]{1,0:T(8,128)(2,1)S(1)} %collective-permute-done.8) | copy-start | bytes 884740
  335.8 18.1 %copy-start.43 = (bf16[192,768]{1,0:T(8,128)(2,1)}, bf16[192,768]{1,0:T(8,128)(2,1)S(1)}, u32[]{:S(2)}) copy-start(bf16[192,768]{1,0:T(8,128)(2,1)S(1)} %collective-permute-done.9) | copy-start | bytes 884740
  359.5 1.8 collective-permute-start.22
  359.6 6.6 %collective-permute-start.11 = (bf16[8,48,768]{2,1,0:T(8,128)(2,1)}, bf16[8,48,768]{2,1,0:T(8,128)(2,1)S(1)}, u32[]{:S(2)}, u32[]{:S(2)}) collective-permute-start(bf16[8,48,768]{2,1,0:T(8,128)(2,1)} %copy-done.25), channel_id=1, source_target_pairs={{0,1},{1,0},{2,3},{3,2},{4,5},{5,4},{6,7},{7,6},{8,9},{9,8},{10,11... | collective-permute-start | bytes 1769480 | tf_op jit(solution)/shard_map/ppermute | solution.py:178
  361.3 4.0 collective-permute-start.23
  366.0 13.7 %collective-permute-start.24 = (f32[72,128]{1,0:T(8,128)}, f32[72,128]{1,0:T(8,128)}, u32[]{:S(2)}, u32[]{:S(2)}) collective-permute-start(f32[72,128]{1,0:T(8,128)} %fusion.115), channel_id=1, source_target_pairs={{0,4},{1,5},{2,6},{3,7},{4,0},{5,1},{6,2},{7,3},{8,12},{9,13},{10,... | collective-permute-start | bytes 110600 | tf_op jit(solution)/shard_map/ppermute | solution.py:75
  377.3 25.8 %collective-permute-start.12 = (bf16[8,48,2304]{2,1,0:T(8,128)(2,1)}, bf16[8,48,2304]{2,1,0:T(8,128)(2,1)}, u32[]{:S(2)}, u32[]{:S(2)}) collective-permute-start(bf16[8,48,2304]{2,1,0:T(8,128)(2,1)} %get-tuple-element.135), channel_id=1, source_target_pairs={{0,1},{1,0},{2,3},{3,2},{4,5},{5,4},{6,7},{7,6},{8,9},{9,8},{10,11... | collective-permute-start | bytes 5308424 | tf_op jit(solution)/shard_map/ppermute | solution.py:178
  380.5 5.0 collective-permute-start.25
  391.7 8.5 %collective-permute-start.26 = (bf16[4,48,768]{2,1,0:T(8,128)(2,1)S(1)}, bf16[4,48,768]{2,1,0:T(8,128)(2,1)S(1)}, u32[]{:S(2)}, u32[]{:S(2)}) collective-permute-start(bf16[4,48,768]{2,1,0:T(8,128)(2,1)S(1)} %get-tuple-element.192), channel_id=1, source_target_pairs={{0,2},{1,3},{2,0},{3,1},{4,6},{5,7},{6,4},{7,5},{8,10},{9,11},{10,... | collective-permute-start | bytes 884744 | tf_op jit(solution)/shard_map/ppermute | solution.py:189
  393.9 14.8 %collective-permute-start.30 = (bf16[48,3072]{1,0:T(8,128)(2,1)S(1)}, bf16[48,3072]{1,0:T(8,128)(2,1)S(1)}, u32[]{:S(2)}, u32[]{:S(2)}) collective-permute-start(bf16[48,3072]{1,0:T(8,128)(2,1)S(1)} %get-tuple-element.178), channel_id=1, source_target_pairs={{0,4},{1,5},{2,6},{3,7},{4,0},{5,1},{6,2},{7,3},{8,12},{9,13},{10,... | collective-permute-start | bytes 884744 | tf_op jit(solution)/shard_map/ppermute | solution.py:199
  396.1 21.3 %collective-permute-start.31 = (bf16[48,3072]{1,0:T(8,128)(2,1)S(1)}, bf16[48,3072]{1,0:T(8,128)(2,1)S(1)}, u32[]{:S(2)}, u32[]{:S(2)}) collective-permute-start(bf16[48,3072]{1,0:T(8,128)(2,1)S(1)} %get-tuple-element.180), channel_id=1, source_target_pairs={{0,8},{1,9},{2,10},{3,11},{4,12},{5,13},{6,14},{7,15},{8,0},{9,1},... | collective-permute-start | bytes 884744 | tf_op jit(solution)/shard_map/ppermute | solution.py:199
  396.5 31.2 %collective-permute-start.32 = (bf16[48,3072]{1,0:T(8,128)(2,1)S(1)}, bf16[48,3072]{1,0:T(8,128)(2,1)S(1)}, u32[]{:S(2)}, u32[]{:S(2)}) collective-permute-start(bf16[48,3072]{1,0:T(8,128)(2,1)S(1)} %get-tuple-element.179), channel_id=1, source_target_pairs={{0,12},{1,13},{2,14},{3,15},{4,8},{5,9},{6,10},{7,11},{8,4},{9,5},... | collective-permute-start | bytes 884744 | tf_op jit(solution)/shard_map/ppermute | solution.py:199
  397.7 44.8 %slice-start.2 = ((s8[4718592]{0:T(1024)(128)(4,1)}), s8[524288]{0:T(1024)(128)(4,1)S(1)}, s32[]{:S(2)}) async-start(s8[4718592]{0:T(1024)(128)(4,1)} %bitcast.236), calls=%async_computation.5 | async-start | bytes 1048576
  400.3 31.0 %collective-permute-start.27 = (bf16[48,768]{1,0:T(8,128)(2,1)S(1)}, bf16[48,768]{1,0:T(8,128)(2,1)S(1)}, u32[]{:S(2)}, u32[]{:S(2)}) collective-permute-start(bf16[48,768]{1,0:T(8,128)(2,1)S(1)} %get-tuple-element.196), channel_id=1, source_target_pairs={{0,4},{1,5},{2,6},{3,7},{4,0},{5,1},{6,2},{7,3},{8,12},{9,13},{10,... | collective-permute-start | bytes 221192 | tf_op jit(solution)/shard_map/ppermute | solution.py:199
  403.2 28.1 %collective-permute-start.28 = (bf16[48,768]{1,0:T(8,128)(2,1)S(1)}, bf16[48,768]{1,0:T(8,128)(2,1)S(1)}, u32[]{:S(2)}, u32[]{:S(2)}) collective-permute-start(bf16[48,768]{1,0:T(8,128)(2,1)S(1)} %get-tuple-element.198), channel_id=1, source_target_pairs={{0,8},{1,9},{2,10},{3,11},{4,12},{5,13},{6,14},{7,15},{8,0},{9,1},... | collective-permute-start | bytes 221192 | tf_op jit(solution)/shard_map/ppermute | solution.py:199
  406.1 29.6 %copy-start.11 = (bf16[8,48,2304]{2,1,0:T(8,128)(2,1)S(1)}, bf16[8,48,2304]{2,1,0:T(8,128)(2,1)}, u32[]{:S(2)}) copy-start(bf16[8,48,2304]{2,1,0:T(8,128)(2,1)} %copy-done.10) | copy-start | bytes 5308420
  408.7 33.8 %slice-start.3 = ((s8[4718592]{0:T(1024)(128)(4,1)}), s8[4194304]{0:T(1024)(128)(4,1)S(1)}, s32[]{:S(2)}) async-start(s8[4718592]{0:T(1024)(128)(4,1)} %bitcast.236), calls=%async_computation.6 | async-start | bytes 8388608
  408.7 22.5 %collective-permute-start.29 = (bf16[48,768]{1,0:T(8,128)(2,1)S(1)}, bf16[48,768]{1,0:T(8,128)(2,1)S(1)}, u32[]{:S(2)}, u32[]{:S(2)}) collective-permute-start(bf16[48,768]{1,0:T(8,128)(2,1)S(1)} %get-tuple-element.197), channel_id=1, source_target_pairs={{0,12},{1,13},{2,14},{3,15},{4,8},{5,9},{6,10},{7,11},{8,4},{9,5},... | collective-permute-start | bytes 221192 | tf_op jit(solution)/shard_map/ppermute | solution.py:199
  417.4 12.3 %collective-permute-start.33 = (bf16[128,768]{1,0:T(8,128)(2,1)S(1)}, bf16[128,768]{1,0:T(8,128)(2,1)S(1)}, u32[]{:S(2)}, u32[]{:S(2)}) collective-permute-start(bf16[128,768]{1,0:T(8,128)(2,1)S(1)} %dynamic-slice_convert_fusion), channel_id=1, source_target_pairs={{0,1},{1,0},{2,3},{3,2},{4,5},{5,4},{6,7},{7,6},{8,9},{9,8},{10,11... | collective-permute-start | bytes 589832 | tf_op jit(solution)/shard_map/ppermute | solution.py:224
  429.8 5.7 %collective-permute-start.34 = (bf16[128,768]{1,0:T(8,128)(2,1)S(1)}, bf16[128,768]{1,0:T(8,128)(2,1)S(1)}, u32[]{:S(2)}, u32[]{:S(2)}) collective-permute-start(bf16[128,768]{1,0:T(8,128)(2,1)S(1)} %fusion.87), channel_id=1, source_target_pairs={{0,2},{1,3},{2,0},{3,1},{4,6},{5,7},{6,4},{7,5},{8,10},{9,11},{10,... | collective-permute-start | bytes 589832 | tf_op jit(solution)/shard_map/ppermute | solution.py:227
  432.0 20.1 %collective-permute-start.17 = (bf16[8,48,1536]{2,1,0:T(8,128)(2,1)S(1)}, bf16[8,48,1536]{2,1,0:T(8,128)(2,1)S(1)}, u32[]{:S(2)}, u32[]{:S(2)}) collective-permute-start(bf16[8,48,1536]{2,1,0:T(8,128)(2,1)S(1)} %get-tuple-element.142), channel_id=1, source_target_pairs={{0,1},{1,0},{2,3},{3,2},{4,5},{5,4},{6,7},{7,6},{8,9},{9,8},{10,11... | collective-permute-start | bytes 3538952 | tf_op jit(solution)/shard_map/ppermute | solution.py:178
  435.6 6.7 %collective-permute-start.35 = (bf16[128,768]{1,0:T(8,128)(2,1)S(1)}, bf16[128,768]{1,0:T(8,128)(2,1)S(1)}, u32[]{:S(2)}, u32[]{:S(2)}) collective-permute-start(bf16[128,768]{1,0:T(8,128)(2,1)S(1)} %fusion.70), channel_id=1, source_target_pairs={{0,4},{1,5},{2,6},{3,7},{4,0},{5,1},{6,2},{7,3},{8,12},{9,13},{10,... | collective-permute-start | bytes 589832 | tf_op jit(solution)/shard_map/ppermute | solution.py:227
  437.7 22.6 %collective-permute-start.13 = (bf16[4,48,2304]{2,1,0:T(8,128)(2,1)S(1)}, bf16[4,48,2304]{2,1,0:T(8,128)(2,1)S(1)}, u32[]{:S(2)}, u32[]{:S(2)}) collective-permute-start(bf16[4,48,2304]{2,1,0:T(8,128)(2,1)S(1)} %get-tuple-element.172), channel_id=1, source_target_pairs={{0,2},{1,3},{2,0},{3,1},{4,6},{5,7},{6,4},{7,5},{8,10},{9,11},{10,... | collective-permute-start | bytes 2654216 | tf_op jit(solution)/shard_map/ppermute | solution.py:189
  442.4 7.5 %collective-permute-start.36 = (bf16[128,768]{1,0:T(8,128)(2,1)S(1)}, bf16[128,768]{1,0:T(8,128)(2,1)S(1)}, u32[]{:S(2)}, u32[]{:S(2)}) collective-permute-start(bf16[128,768]{1,0:T(8,128)(2,1)S(1)} %get-tuple-element.159), channel_id=1, source_target_pairs={{0,8},{1,9},{2,10},{3,11},{4,12},{5,13},{6,14},{7,15},{8,0},{9,1},... | collective-permute-start | bytes 589832 | tf_op jit(solution)/shard_map/ppermute | solution.py:227
  449.9 14.1 %collective-permute-start.37 = (bf16[128,768]{1,0:T(8,128)(2,1)S(1)}, bf16[128,768]{1,0:T(8,128)(2,1)S(1)}, u32[]{:S(2)}, u32[]{:S(2)}) collective-permute-start(bf16[128,768]{1,0:T(8,128)(2,1)S(1)} %fusion.71), channel_id=1, source_target_pairs={{0,16},{16,0},{1,17},{17,1},{2,18},{18,2},{3,19},{19,3},{4,20},{20... | collective-permute-start | bytes 589832 | tf_op jit(solution)/shard_map/ppermute | solution.py:61
  452.4 16.6 %collective-permute-start.18 = (bf16[4,48,1536]{2,1,0:T(8,128)(2,1)S(1)}, bf16[4,48,1536]{2,1,0:T(8,128)(2,1)S(1)}, u32[]{:S(2)}, u32[]{:S(2)}) collective-permute-start(bf16[4,48,1536]{2,1,0:T(8,128)(2,1)S(1)} %get-tuple-element.182), channel_id=1, source_target_pairs={{0,2},{1,3},{2,0},{3,1},{4,6},{5,7},{6,4},{7,5},{8,10},{9,11},{10,... | collective-permute-start | bytes 1769480 | tf_op jit(solution)/shard_map/ppermute | solution.py:189
  460.4 10.4 %collective-permute-start.14 = (bf16[48,2304]{1,0:T(8,128)(2,1)S(1)}, bf16[48,2304]{1,0:T(8,128)(2,1)S(1)}, u32[]{:S(2)}, u32[]{:S(2)}) collective-permute-start(bf16[48,2304]{1,0:T(8,128)(2,1)S(1)} %get-tuple-element.186), channel_id=1, source_target_pairs={{0,4},{1,5},{2,6},{3,7},{4,0},{5,1},{6,2},{7,3},{8,12},{9,13},{10,... | collective-permute-start | bytes 663560 | tf_op jit(solution)/shard_map/ppermute | solution.py:199
  462.5 12.0 %collective-permute-start.15 = (bf16[48,2304]{1,0:T(8,128)(2,1)S(1)}, bf16[48,2304]{1,0:T(8,128)(2,1)S(1)}, u32[]{:S(2)}, u32[]{:S(2)}) collective-permute-start(bf16[48,2304]{1,0:T(8,128)(2,1)S(1)} %get-tuple-element.188), channel_id=1, source_target_pairs={{0,8},{1,9},{2,10},{3,11},{4,12},{5,13},{6,14},{7,15},{8,0},{9,1},... | collective-permute-start | bytes 663560 | tf_op jit(solution)/shard_map/ppermute | solution.py:199
  462.9 22.1 %collective-permute-start.16 = (bf16[48,2304]{1,0:T(8,128)(2,1)S(1)}, bf16[48,2304]{1,0:T(8,128)(2,1)S(1)}, u32[]{:S(2)}, u32[]{:S(2)}) collective-permute-start(bf16[48,2304]{1,0:T(8,128)(2,1)S(1)} %get-tuple-element.187), channel_id=1, source_target_pairs={{0,12},{1,13},{2,14},{3,15},{4,8},{5,9},{6,10},{7,11},{8,4},{9,5},... | collective-permute-start | bytes 663560 | tf_op jit(solution)/shard_map/ppermute | solution.py:199
  464.1 21.7 %collective-permute-start.38 = (bf16[128,768]{1,0:T(8,128)(2,1)S(1)}, bf16[128,768]{1,0:T(8,128)(2,1)S(1)}, u32[]{:S(2)}, u32[]{:S(2)}) collective-permute-start(bf16[128,768]{1,0:T(8,128)(2,1)S(1)} %get-tuple-element.157), channel_id=1, source_target_pairs={{0,1},{1,0},{2,3},{3,2},{4,5},{5,4},{6,7},{7,6},{8,9},{9,8},{10,11... | collective-permute-start | bytes 589832 | tf_op jit(solution)/shard_map/ppermute | solution.py:230
  469.0 17.8 %collective-permute-start.19 = (bf16[48,1536]{1,0:T(8,128)(2,1)S(1)}, bf16[48,1536]{1,0:T(8,128)(2,1)S(1)}, u32[]{:S(2)}, u32[]{:S(2)}) collective-permute-start(bf16[48,1536]{1,0:T(8,128)(2,1)S(1)} %get-tuple-element.193), channel_id=1, source_target_pairs={{0,4},{1,5},{2,6},{3,7},{4,0},{5,1},{6,2},{7,3},{8,12},{9,13},{10,... | collective-permute-start | bytes 442376 | tf_op jit(solution)/shard_map/ppermute | solution.py:199
  470.8 16.0 %collective-permute-start.20 = (bf16[48,1536]{1,0:T(8,128)(2,1)S(1)}, bf16[48,1536]{1,0:T(8,128)(2,1)S(1)}, u32[]{:S(2)}, u32[]{:S(2)}) collective-permute-start(bf16[48,1536]{1,0:T(8,128)(2,1)S(1)} %get-tuple-element.195), channel_id=1, source_target_pairs={{0,8},{1,9},{2,10},{3,11},{4,12},{5,13},{6,14},{7,15},{8,0},{9,1},... | collective-permute-start | bytes 442376 | tf_op jit(solution)/shard_map/ppermute | solution.py:199
  474.5 13.6 %collective-permute-start.21 = (bf16[48,1536]{1,0:T(8,128)(2,1)S(1)}, bf16[48,1536]{1,0:T(8,128)(2,1)S(1)}, u32[]{:S(2)}, u32[]{:S(2)}) collective-permute-start(bf16[48,1536]{1,0:T(8,128)(2,1)S(1)} %get-tuple-element.194), channel_id=1, source_target_pairs={{0,12},{1,13},{2,14},{3,15},{4,8},{5,9},{6,10},{7,11},{8,4},{9,5},... | collective-permute-start | bytes 442376 | tf_op jit(solution)/shard_map/ppermute | solution.py:199
  (36 other events, 139.5 us)
Sparse Core Ops, SparseCore 0:
  10.8 67.2 all-gather.3
  80.4 51.8 all-gather.5
  134.6 51.6 all-gather.7
